TPU v7x, 128 devices: a whole 4x4x4 slice. The times are simulated.
128 devices in a mesh: pipe: 2 (over core), ctx: 64 (over x, z, y).
Axes of the slice: x: 4, y: 4, z: 4, core: 2. Of those that a mesh axis runs over, the one named last changes fastest.
Arguments:
- saved: bfloat16 [2, 8192, 4096], P('pipe', 'ctx'), may hold values from -6 to 6
- grad_out: bfloat16 [8192, 4096], P('ctx'), may hold values from -6 to 6
- route_blocks: int32 [2, 64, 2], P('pipe', 'ctx'), may hold values from 0 to 31, as said below
- route_dest: int32 [2, 64, 2], P('pipe', 'ctx'), may hold values from -1 to 63, as said below
- gain: float32 [2, 4096], P('pipe'), may hold values from 0.5 to 2
- w_router: bfloat16 [2, 4096], P('pipe'), may hold values from -0.09375 to 0.09375
- w_gate: bfloat16 [2, 14336, 4096], P('pipe', 'ctx'), may hold values from -0.09375 to 0.09375
- w_up: bfloat16 [2, 14336, 4096], P('pipe', 'ctx'), may hold values from -0.09375 to 0.09375
- w_down: bfloat16 [2, 14336, 4096], P('pipe', 'ctx'), may hold values from -0.046875 to 0.046875
Outputs:
- grad_inputs: bfloat16 [2, 8192, 4096], P('pipe', 'ctx')
- grad_gate: float32 [2, 14336, 4096], P('pipe', 'ctx')
- grad_up: float32 [2, 14336, 4096], P('pipe', 'ctx')
- grad_down: float32 [2, 14336, 4096], P('pipe', 'ctx')
- grad_gain: float32 [2, 4096], P('pipe')
- grad_router: float32 [2, 4096], P('pipe')
Inputs may be any that keep to these rules, and one draw needn't show every extreme that they name: In each row route_blocks[l, o, :] the 2 entries are distinct block numbers of owner o; only slots whose route_dest entry is not -1 are routed. In each row route_dest[l, o, :] the used slots come first: blocks that owner o works on itself (entry o), then blocks handed to the next owner (entry (o + 1) mod 64), then -1. An owner keeps at most 1 block and hands on at most 1; every device works on exactly 1 block of each layer, so 64 * 1 blocks are routed in each layer; in each layer some owner uses all 2 slots, keeping 1 and handing on 1.
All inputs are finite; a program needn't handle non-finite values.
Results may differ from a plain program's by a relative error of at most 0.007.
Values may be sent and summed in bfloat16 or wider, within the bound.
A program may use at most 128 MiB of HBM per device.

v0:
```python
import jax
import jax.numpy as jnp
from jax import lax
from jax.sharding import PartitionSpec as P

BLOCK = 4


EPSILON = 1e-05


def passed_along(block, axis, distance):
    devices = range(lax.axis_size(axis))
    route = [(i - distance, i) for i in devices if i - distance in devices]
    return lax.ppermute(block, axis, route)


def silu_parts(gate_pre):
    sigma = jax.nn.sigmoid(gate_pre)
    return (gate_pre * sigma, sigma * (1.0 + gate_pre * (1.0 - sigma)))


def contract_last(left_side, right_side):
    return lax.dot_general(
        left_side, right_side, (((1,), (1,)), ((), ())), preferred_element_type=jnp.float32
    )


def contract_first(left_side, right_side):
    return lax.dot_general(
        left_side, right_side, (((0,), (0,)), ((), ())), preferred_element_type=jnp.float32
    )


def on_device(saved, grad_out, route_blocks, route_dest, gain, w_router, w_gate, w_up, w_down):
    sections = lax.axis_size("pipe")
    section_index = lax.axis_index("pipe")
    peer_count = lax.axis_size("ctx")
    tokens = saved[0]
    tok_rows, model_dim = tokens.shape
    blocks = route_blocks[0, 0]
    targets = route_dest[0, 0]
    slot_count = blocks.shape[0]
    block_count = tok_rows // BLOCK
    gain_row = gain[0]
    router_row = w_router[0]
    gate_local = w_gate[0]
    up_local = w_up[0]
    down_local = w_down[0]
    ff_local = gate_local.shape[0]
    used_slot = targets >= 0
    used_rows = used_slot[:, None, None]
    picked = tokens.reshape(block_count, BLOCK, model_dim)[blocks]
    picked_f = picked.astype(jnp.float32)
    inverse = lax.rsqrt(jnp.mean(picked_f * picked_f, axis=2, keepdims=True) + EPSILON)
    normal_hat = picked_f * inverse
    normed = jnp.where(used_rows, normal_hat * gain_row, 0.0).astype(jnp.bfloat16)
    logits = jnp.dot(
        picked.reshape(slot_count * BLOCK, model_dim),
        router_row,
        preferred_element_type=jnp.float32,
    )
    router_prob = jax.nn.sigmoid(logits.reshape(slot_count, BLOCK))
    zero_weights = jnp.zeros((ff_local, model_dim), jnp.float32)
    weight_acc = (zero_weights, zero_weights, zero_weights)
    stat_gain = jnp.zeros((model_dim,), jnp.float32)
    stat_router = jnp.zeros((model_dim,), jnp.float32)
    outcome = jnp.zeros_like(tokens)
    latest = grad_out
    for tick_step in range(sections):
        active = section_index == sections - 1 - tick_step
        if tick_step > 0:
            latest = passed_along(latest, "pipe", -1)
        incoming = jnp.where(active, latest, jnp.zeros_like(latest))
        one_weight_acc = weight_acc
        upstream_rows = incoming.reshape(block_count, BLOCK, model_dim)[blocks]
        scaled = jnp.where(
            used_rows, router_prob[:, :, None] * upstream_rows.astype(jnp.float32), 0.0
        ).astype(jnp.bfloat16)
        normed_buffer = normed.reshape(slot_count * BLOCK, model_dim)
        row_count = normed_buffer.shape[0]
        initial = one_weight_acc + (
            jnp.zeros((peer_count * row_count, model_dim), jnp.float32),
            jnp.zeros((peer_count * row_count,), jnp.float32),
        )
        acc_gate, acc_up, acc_down, grads_all, sums_all = initial
        normed_part = lax.all_gather(normed_buffer, "ctx", axis=0, tiled=True)
        scaled_part = lax.all_gather(
            scaled.reshape(slot_count * BLOCK, model_dim), "ctx", axis=0, tiled=True
        )
        gate_pre = contract_last(normed_part, gate_local)
        up_value = contract_last(normed_part, up_local)
        activated, slope_term = silu_parts(gate_pre)
        hidden = (activated * up_value).astype(jnp.bfloat16)
        hidden_grad = contract_last(scaled_part, down_local)
        sums_part = jnp.sum(hidden_grad * hidden.astype(jnp.float32), axis=1)
        gate_grad = (hidden_grad * up_value * slope_term).astype(jnp.bfloat16)
        up_grad = (hidden_grad * activated).astype(jnp.bfloat16)
        acc_down = acc_down + contract_first(hidden, scaled_part)
        acc_gate = acc_gate + contract_first(gate_grad, normed_part)
        acc_up = acc_up + contract_first(up_grad, normed_part)
        grads_part = jnp.dot(gate_grad, gate_local, preferred_element_type=jnp.float32) + jnp.dot(
            up_grad, up_local, preferred_element_type=jnp.float32
        )
        grads_all = grads_part
        sums_all = sums_part
        grads_mine = lax.psum_scatter(grads_all, "ctx", scatter_dimension=0, tiled=True)
        sums_mine = lax.psum_scatter(sums_all, "ctx", scatter_dimension=0, tiled=True)
        one_weight_acc = (acc_gate, acc_up, acc_down)
        normed_grad = grads_mine.reshape(slot_count, BLOCK, model_dim)
        row_sums = sums_mine.reshape(slot_count, BLOCK)
        logit_grad = row_sums * (1.0 - router_prob)
        hat_grad = normed_grad * gain_row
        norm_part = inverse * (
            hat_grad - normal_hat * jnp.mean(hat_grad * normal_hat, axis=2, keepdims=True)
        )
        row_delta = jnp.where(
            used_rows, norm_part + logit_grad[:, :, None] * router_row.astype(jnp.float32), 0.0
        )
        block_grads = (
            incoming.reshape(block_count, BLOCK, model_dim)
            .astype(jnp.float32)
            .at[blocks]
            .add(row_delta)
        )
        input_grad = block_grads.reshape(tok_rows, model_dim).astype(jnp.bfloat16)
        gain_part = jnp.sum(jnp.where(used_rows, normed_grad * normal_hat, 0.0), axis=(0, 1))
        router_part = jnp.sum(
            jnp.where(used_rows, logit_grad[:, :, None] * picked_f, 0.0), axis=(0, 1)
        )
        input_grad, weight_acc, gain_part, router_part = (
            input_grad,
            one_weight_acc,
            gain_part,
            router_part,
        )
        gain_part, router_part = lax.psum((gain_part, router_part), "ctx")
        stat_gain = stat_gain + gain_part
        stat_router = stat_router + router_part
        outcome = jnp.where(active, input_grad, outcome)
        latest = input_grad
    return (
        outcome[None],
        weight_acc[0][None],
        weight_acc[1][None],
        weight_acc[2][None],
        stat_gain[None],
        stat_router[None],
    )


def solution(mesh):
    in_specs = (
        P("pipe", "ctx", None),
        P("ctx", None),
        P("pipe", "ctx", None),
        P("pipe", "ctx", None),
        P("pipe", None),
        P("pipe", None),
        P("pipe", "ctx", None),
        P("pipe", "ctx", None),
        P("pipe", "ctx", None),
    )
    out_specs = (
        P("pipe", "ctx", None),
        P("pipe", "ctx", None),
        P("pipe", "ctx", None),
        P("pipe", "ctx", None),
        P("pipe", None),
        P("pipe", None),
    )
    return jax.shard_map(
        on_device, mesh=mesh, in_specs=in_specs, out_specs=out_specs, check_vma=False
    )
```

profile of v0, /device:TPU:0, one launch (start us, length us, event | category | flops | bytes accessed | tf_op | source)
XLA Modules:
  0.0 1354.4 jit_solution(362525777571576851)
XLA Ops:
  17.1 71.5 %all-gather.6.cloned.1.call-done = bf16[512,4096]{1,0:T(8,128)(2,1)} async-done(((bf16[8,4096]{1,0:T(8,128)(2,1)}), bf16[512,4096]{1,0:T(8,128)(2,1)}) %all-gather.6.cloned.1.call-update) | async-done | bytes 4194320 | tf_op jit(solution)/shard_map/all_gather | solution.py:87
  88.6 5.1 fusion.11
  93.8 2.3 fusion.7
  96.0 62.5 %all-gather.4.cloned.1.call-done = bf16[512,4096]{1,0:T(8,128)(2,1)} async-done(((bf16[8,4096]{1,0:T(8,128)(2,1)}), bf16[512,4096]{1,0:T(8,128)(2,1)}) %all-gather.4.cloned.1.call-update) | async-done | bytes 4194320 | tf_op jit(solution)/shard_map/all_gather | solution.py:88
  158.5 5.1 fusion.17
  165.2 4.6 convolution_add_fusion.1
  174.1 175.2 %all-reduce = f32[512]{0:T(512)S(1)} all-reduce(f32[512]{0:T(512)} %get-tuple-element.14), channel_id=3, replica_groups=mesh['pipe'=2,'ctx'=64] {'ctx'}, use_global_device_ids=true, to_apply=%region_4.5.clone | all-reduce | flops 512 | bytes 4096
  350.2 185.6 %reduce-scatter.3.cloned.1.call-done = f32[8,4096]{1,0:T(8,128)} async-done(((f32[512,4096]{1,0:T(8,128)}), f32[8,4096]{1,0:T(8,128)}) %reduce-scatter.3.cloned.1.call-update) | async-done | bytes 131088 | tf_op jit(solution)/shard_map/reduce_scatter | solution.py:107
  539.3 2.3 scatter_fusion
  546.0 3.5 collective-permute-done
  556.7 63.7 %all-gather.8.cloned.1.call-done = bf16[512,4096]{1,0:T(8,128)(2,1)} async-done(((bf16[8,4096]{1,0:T(8,128)(2,1)}), bf16[512,4096]{1,0:T(8,128)(2,1)}) %all-gather.8.cloned.1.call-update) | async-done | bytes 4194320 | tf_op jit(solution)/shard_map/all_gather | solution.py:88
  620.4 5.1 multiply_convert_fusion
  627.1 4.5 convolution_add_fusion
  631.7 5.3 fusion.25
  637.0 3.0 fusion.24
  640.0 3.0 fusion.23
  644.6 175.0 %all-reduce.1 = f32[512]{0:T(512)S(1)} all-reduce(f32[512]{0:T(512)S(1)} %copy-done.35), channel_id=5, replica_groups=mesh['pipe'=2,'ctx'=64] {'ctx'}, use_global_device_ids=true, to_apply=%region_9.10.clone | all-reduce | flops 512 | bytes 4096
  819.8 6.4 fusion
  826.3 3.1 fusion.1
  829.4 3.1 fusion.2
  832.5 164.8 %reduce-scatter.5.cloned.1.call-done = f32[8,4096]{1,0:T(8,128)} async-done(((f32[512,4096]{1,0:T(8,128)}), f32[8,4096]{1,0:T(8,128)}) %reduce-scatter.5.cloned.1.call-update) | async-done | bytes 131088 | tf_op jit(solution)/shard_map/reduce_scatter | solution.py:107
  999.8 2.2 scatter_fusion.1
  1001.9 2.8 select_select_fusion
  1005.9 342.0 %all-reduce.2 = (f32[4096]{0:T(1024)}, f32[4096]{0:T(1024)}) all-reduce(f32[4096]{0:T(1024)S(1)} %add.94, f32[4096]{0:T(1024)S(1)} %add.95), channel_id=1, replica_groups=mesh['pipe'=2,'ctx'=64] {'ctx'}, use_global_device_ids=true, to_apply=%region_12.13 | all-reduce | flops 8192 | bytes 65536 | tf_op jit(solution)/shard_map/psum | solution.py:137
  (137 shorter events, 37.9 us)
Async XLA Ops:
  7.2 86.6 %copy-start = (bf16[1,224,4096]{2,1,0:T(8,128)(2,1)S(1)}, bf16[1,224,4096]{2,1,0:T(8,128)(2,1)}, u32[]{:S(2)}) copy-start(bf16[1,224,4096]{2,1,0:T(8,128)(2,1)} %param.15) | copy-start | bytes 5505028
  7.2 7.6 copy-start.36
  7.2 8.3 copy-start.15
  7.2 81.4 %all-gather.6.cloned.1.call-start = ((), (), s32[]{:S(2)}) async-start(), calls=%async_computation.3 | async-start | bytes 4259840 | tf_op jit(solution)/shard_map/all_gather | solution.py:87
  10.4 83.3 %copy-start.28 = (f32[8]{0:T(128)}, f32[8]{0:T(128)S(1)}, u32[]{:S(2)}) copy-start(f32[8]{0:T(128)S(1)} %rsqrt.13) | copy-start | bytes 100
  11.6 82.1 %copy-start.34 = (f32[8]{0:T(128)}, f32[8]{0:T(128)S(1)}, u32[]{:S(2)}) copy-start(f32[8]{0:T(128)S(1)} %mul.197) | copy-start | bytes 100
  15.5 78.2 %copy-start.25 = (pred[8]{0:T(512)(128)(4,1)}, pred[8]{0:T(512)(128)(4,1)S(1)}, u32[]{:S(2)}) copy-start(pred[8]{0:T(512)(128)(4,1)S(1)} %broadcast_in_dim.87) | copy-start | bytes 28
  16.3 142.3 %all-gather.4.cloned.1.call-start = ((), (), s32[]{:S(2)}) async-start(), calls=%async_computation.2 | async-start | bytes 4259840 | tf_op jit(solution)/shard_map/all_gather | solution.py:88
  17.0 518.8 %reduce-scatter.3.cloned.1.call-start = ((), (), s32[]{:S(2)}) async-start(), calls=%async_computation.4 | async-start | bytes 8519680 | tf_op jit(solution)/shard_map/reduce_scatter | solution.py:107
  169.8 450.6 %all-gather.8.cloned.1.call-start = ((), (), s32[]{:S(2)}) async-start(), calls=%async_computation.5 | async-start | bytes 4259840 | tf_op jit(solution)/shard_map/all_gather | solution.py:88
  172.2 367.1 %copy-start.16 = (f32[4096]{0:T(1024)}, f32[4096]{0:T(1024)S(1)}, u32[]{:S(2)}) copy-start(f32[4096]{0:T(1024)S(1)} %convert_element_type.110) | copy-start | bytes 49156
  350.2 189.1 %copy-start.19 = (f32[2,4]{1,0:T(2,128)}, f32[2,4]{1,0:T(2,128)S(1)}, u32[]{:S(2)}) copy-start(f32[2,4]{1,0:T(2,128)S(1)} %subtract_multiply_fusion.1) | copy-start | bytes 100
  544.7 4.8 collective-permute-start
  556.5 440.8 %reduce-scatter.5.cloned.1.call-start = ((), (), s32[]{:S(2)}) async-start(), calls=%async_computation.6 | async-start | bytes 8519680 | tf_op jit(solution)/shard_map/reduce_scatter | solution.py:107
  640.0 179.7 %copy-start.24 = (f32[1,2,4]{2,0,1:T(1,128)S(1)}, f32[1,2,4]{2,0,1:T(1,128)}, u32[]{:S(2)}) copy-start(f32[1,2,4]{2,0,1:T(1,128)} %copy-done.23) | copy-start | bytes 100
  819.8 6.5 copy-start.4
  829.3 167.9 %copy-start.26 = (pred[8]{0:T(512)(128)(4,1)S(1)}, pred[8]{0:T(512)(128)(4,1)}, u32[]{:S(2)}) copy-start(pred[8]{0:T(512)(128)(4,1)} %copy-done.25) | copy-start | bytes 28
  829.3 167.9 %copy-start.29 = (f32[8]{0:T(128)S(1)}, f32[8]{0:T(128)}, u32[]{:S(2)}) copy-start(f32[8]{0:T(128)} %copy-done.28) | copy-start | bytes 100
  829.3 170.1 %copy-start.17 = (f32[4096]{0:T(1024)S(1)}, f32[4096]{0:T(1024)}, u32[]{:S(2)}) copy-start(f32[4096]{0:T(1024)} %copy-done.16) | copy-start | bytes 49156
  829.4 170.1 %copy-start.20 = (f32[2,4]{1,0:T(2,128)S(1)}, f32[2,4]{1,0:T(2,128)}, u32[]{:S(2)}) copy-start(f32[2,4]{1,0:T(2,128)} %copy-done.19) | copy-start | bytes 100
  829.4 170.1 %copy-start.22 = (f32[2,4]{1,0:T(2,128)S(1)}, f32[2,4]{1,0:T(2,128)}, u32[]{:S(2)}) copy-start(f32[2,4]{1,0:T(2,128)} %copy-done.21) | copy-start | bytes 100
  829.4 170.1 %copy-start.33 = (pred[2]{0:T(512)(128)(4,1)S(1)}, pred[2]{0:T(512)(128)(4,1)}, u32[]{:S(2)}) copy-start(pred[2]{0:T(512)(128)(4,1)} %copy-done.32) | copy-start | bytes 10
  829.4 170.4 %copy-start.31 = (s32[2]{0:T(128)S(1)}, s32[2]{0:T(128)}, u32[]{:S(2)}) copy-start(s32[2]{0:T(128)} %copy-done.30) | copy-start | bytes 28
  999.8 348.1 %copy-start.1 = (bf16[1,224,4096]{2,1,0:T(8,128)(2,1)S(1)}, bf16[1,224,4096]{2,1,0:T(8,128)(2,1)}, u32[]{:S(2)}) copy-start(bf16[1,224,4096]{2,1,0:T(8,128)(2,1)} %param.15) | copy-start | bytes 5505028
  (19 other events, 67.5 us)
Sparse Core Ops, SparseCore 0:
  16.4 72.1 all-gather.5
  92.0 66.4 all-gather.3
  169.9 365.8 reduce-scatter.2
  556.6 63.7 all-gather.7
  631.8 365.4 reduce-scatter.4
where the time goes:
time: 1360 us; the launch traced here: 1350 us
  blocking collectives  692 us (51%)
  waiting for transfers between devices  552 us (41%)
  matrix products  54.3 us (4%)
  other arithmetic  23.2 us (2%)
  local copies, waits for them, and re-layouts  15.9 us (1%)
  between operations  14.9 us (1%)
    reduce_scatter x2, waiting for transfers between devices, on_device(): lax.psum_scatter(grads_all, 'ctx', scatter_dimension=0, tiled=True)  350 us
    unnamed x2, blocking collectives  350 us
    psum x1, blocking collectives, on_device(): gain_part, router_part = lax.psum((gain_part, router_part), 'ctx')  342 us
    all_gather x2, waiting for transfers between devices, on_device(): lax.all_gather(scaled.reshape(slot_count * BLOCK, model_dim), 'ctx', axis...  126 us
    all_gather x1, waiting for transfers between devices, on_device(): normed_part = lax.all_gather(normed_buffer, 'ctx', axis=0, tiled=True)  71.5 us
  transfers between devices with their start and end apart: 6, of which 6 were waited for; matrix products, arithmetic and copies ran while one was open for 3% of the time, Pallas kernels for 0%

commit v1 on v0

v1 whole, which is shorter than its diff:
```python
import jax
import jax.numpy as jnp
from jax import lax
from jax.experimental import pallas as pl
from jax.experimental.pallas import tpu as pltpu
from jax.sharding import PartitionSpec as P

BLOCK = 4
EPSILON = 1e-05
RING = 4
OFFS = (1, 2, 3)
QUARTER = 1024
EXTRA = 128
WIDTHS = (384, 384, 384)
FEATS = (384, 384, 256)
STARTS = (0, 384, 768)
ROWS = 16
ORDERS = ((0, 1, 2), (1, 2, 0), (2, 0, 1))
F32 = jnp.float32
BF16 = jnp.bfloat16
MESH = pl.DeviceIdType.MESH


def contract_last(left_side, right_side):
    return lax.dot_general(
        left_side, right_side, (((1,), (1,)), ((), ())), preferred_element_type=F32
    )


def contract_first(left_side, right_side):
    return lax.dot_general(
        left_side, right_side, (((0,), (0,)), ((), ())), preferred_element_type=F32
    )


def hi_lo(value):
    hi = value.astype(BF16).astype(F32)
    return hi, value - hi


def step_kernel(
    bn, up_in, hat_in, gain_in, wr_in, sc, wg_hbm, wu_hbm, wd_hbm,
    go0, go1, go2, so0, so1, so2, hid_o, gg_o, ug_o, nb_o, new_o, st_o,
    up_ref, bs, hn, hs, g0, g1, g2, s0, s1, s2, r0, r1, r2,
    rb00, rb01, rb02, a00, a01, a02, rb10, rb11, rb12, a10, a11, a12, rb20, rb21, rb22,
    u, nb, nbsend, srb, acc, wg, wu, wd,
    hand_send, hand_recv, ag_send, ag_recv, rs_send, rs_recv, st_send, st_recv,
    un_send, un_recv, nb_send, nb_recv, local_sem,
):
    pipe = lax.axis_index("pipe")
    me = lax.axis_index("ctx")
    yy = lax.rem(me, RING)
    quartet = lax.div(me, RING)
    zz = lax.rem(quartet, RING)
    xx = lax.div(quartet, RING)
    at = (yy, xx, zz)
    quartets = RING * RING
    next_base = lax.rem(quartet + 1, quartets) * RING
    prev_last = lax.rem(quartet + quartets - 1, quartets) * RING + RING - 1

    def ring_index(dim, off):
        return lax.rem(at[dim] + RING - off, RING)

    def peer(dim, off):
        pos = list(at)
        pos[dim] = ring_index(dim, off)
        return {"pipe": pipe, "ctx": pos[1] * 16 + pos[2] * 4 + pos[0]}

    def same_pipe(ctx):
        return {"pipe": pipe, "ctx": ctx}

    partner = {"pipe": 1 - pipe, "ctx": me}

    def remote(src, dst, send, recv, device):
        return pltpu.make_async_remote_copy(
            src_ref=src, dst_ref=dst, send_sem=send, recv_sem=recv,
            device_id=device, device_id_type=MESH,
        )

    gs, ss, rs = (g0, g1, g2), (s0, s1, s2), (r0, r1, r2)
    rb0, a0 = (rb00, rb01, rb02), (a00, a01, a02)
    rb1, a1 = (rb10, rb11, rb12), (a10, a11, a12)
    rb2 = (rb20, rb21, rb22)

    weight_copies = [
        pltpu.make_async_copy(src, dst, local_sem.at[i])
        for i, (src, dst) in enumerate(((wg_hbm, wg), (wu_hbm, wu), (wd_hbm, wd)))
    ]
    for copy in weight_copies:
        copy.start()

    barrier = pltpu.get_barrier_semaphore()

    def greet(device):
        pl.semaphore_signal(barrier, inc=1, device_id=device, device_id_type=MESH)

    for dim in range(3):
        for off in OFFS:
            greet(peer(dim, off))
    greet(partner)
    greet(same_pipe(prev_last))

    @pl.when(yy == RING - 1)
    def _():
        for j in range(RING):
            greet(same_pipe(next_base + j))

    pl.semaphore_wait(barrier, 11 + RING * lax.div(yy, RING - 1))

    def hand_copies(src, dst, which):
        return [
            remote(
                src.at[ring_index(0, off)], dst.at[yy + 1],
                hand_send.at[which, off], hand_recv.at[which, off], peer(0, off),
            )
            for off in OFFS
        ]

    def hand_over_copy(src, dst, which, j):
        return remote(
            src.at[j], dst.at[0],
            hand_send.at[which, RING + j], hand_recv.at[which, 0], same_pipe(next_base + j),
        )

    def hand_start(src, dst, which):
        for copy in hand_copies(src, dst, which):
            copy.start()

        @pl.when(yy == RING - 1)
        def _():
            for j in range(RING):
                hand_over_copy(src, dst, which, j).start()

        dst[yy + 1] = src[yy]

    def hand_wait(src, dst, which):
        for copy in hand_copies(src, dst, which):
            copy.wait()
        hand_over_copy(src, dst, which, 0).wait_recv()

        @pl.when(yy == RING - 1)
        def _():
            for j in range(RING):
                hand_over_copy(src, dst, which, j).wait_send()

    def make_tile(held, bufs, widths):
        for k in range(3):
            cols = slice(STARTS[k], STARTS[k] + widths[k])
            b = [held[i, :, cols].astype(F32) for i in range(5)]
            low = lax.broadcasted_iota(jnp.int32, b[0].shape, 0) < BLOCK
            turned = [pltpu.roll(b[i], BLOCK, 0) for i in (0, 2, 4)]
            top = b[1] + jnp.where(low, turned[0], turned[1])
            bottom = b[3] + jnp.where(low, turned[1], turned[2])
            bufs[k][yy, xx, zz] = jnp.concatenate([top, bottom], axis=0).astype(BF16)

    def ag_copies(bufs, which, k, stage):
        dim = ORDERS[k][stage]
        index = tuple(
            slice(None) if d in ORDERS[k][:stage] else at[d] for d in range(3)
        )
        return [
            remote(
                bufs[k].at[index], bufs[k].at[index],
                ag_send.at[which, k, stage, off], ag_recv.at[which, k, stage, off],
                peer(dim, off),
            )
            for off in OFFS
        ]

    def ag_start(bufs, which, k, stage):
        for copy in ag_copies(bufs, which, k, stage):
            copy.start()

    def ag_recv_wait(bufs, which, k, stage):
        for copy in ag_copies(bufs, which, k, stage):
            copy.wait_recv()

    def ag_send_wait(bufs, which):
        for k in range(3):
            for stage in range(3):
                for copy in ag_copies(bufs, which, k, stage):
                    copy.wait_send()

    def make_scaled():
        for q in range(RING):
            bs[q] = (sc[1][:, 0:1] * up_ref[q]).astype(BF16)

    @pl.when(pipe == 1)
    def _():
        up_ref[...] = up_in[...]
        make_scaled()

    hand_start(bn, hn, 0)

    @pl.when(pipe == 1)
    def _():
        hand_start(bs, hs, 1)

    hand_wait(bn, hn, 0)
    make_tile(hn, gs, WIDTHS)
    for k in range(3):
        ag_start(gs, 0, k, 0)

    @pl.when(pipe == 1)
    def _():
        hand_wait(bs, hs, 1)
        make_tile(hs, ss, FEATS)
        for k in range(3):
            ag_start(ss, 1, k, 0)

    for stage in (1, 2):
        for k in range(3):
            ag_recv_wait(gs, 0, k, stage - 1)
            ag_start(gs, 0, k, stage)

        @pl.when(pipe == 1)
        def _(stage=stage):
            for k in range(3):
                ag_recv_wait(ss, 1, k, stage - 1)
                ag_start(ss, 1, k, stage)

    for copy in weight_copies:
        copy.wait()

    def rows_of(bufs, k, q):
        return bufs[k][q, :, :, :, : FEATS[k]].reshape(quartets * ROWS, FEATS[k])

    def columns(k, q):
        return slice(q * QUARTER + STARTS[k], q * QUARTER + STARTS[k] + FEATS[k])

    gathered_out = [
        pltpu.make_async_copy(src, dst, local_sem.at[3 + i])
        for i, (src, dst) in enumerate(zip(gs + ss, (go0, go1, go2, so0, so1, so2)))
    ]

    for k in range(3):
        ag_recv_wait(gs, 0, k, 2)
        gathered_out[k].start()
        gate_sum = None
        up_sum = None
        for q in range(RING):
            rows = rows_of(gs, k, q)
            gate_part = contract_last(rows, wg[:, columns(k, q)])
            up_part = contract_last(rows, wu[:, columns(k, q)])
            gate_sum = gate_part if gate_sum is None else gate_sum + gate_part
            up_sum = up_part if up_sum is None else up_sum + up_part
        if k == 0:
            acc[0] = gate_sum
            acc[1] = up_sum
        else:
            acc[0] += gate_sum
            acc[1] += up_sum

    def nb_copy():
        return remote(nbsend, nb, nb_send, nb_recv, partner)

    @pl.when(pipe == 0)
    def _():
        nb_copy().wait_recv()
        low = lax.broadcasted_iota(jnp.int32, (2 * BLOCK, 1), 0) < BLOCK
        mine = sc[4][:, 0:1]
        same = 1.0 - jnp.minimum(jnp.abs(nb[0, :, QUARTER : QUARTER + 1].astype(F32) - mine), 1.0)
        other = pltpu.roll(nb[0, :, QUARTER:].astype(F32), BLOCK, 0)[:, 0:1]
        cross = 1.0 - jnp.minimum(jnp.abs(other - mine), 1.0)
        for q in range(RING):
            rows = nb[q, :, :QUARTER].astype(F32)
            turned = pltpu.roll(rows, BLOCK, 0)
            kept_rows = (1.0 - same - cross) * up_in[q]
            up_ref[q] = same * rows + cross * turned + kept_rows
        make_scaled()
        hand_start(bs, hs, 1)
        hand_wait(bs, hs, 1)
        make_tile(hs, ss, FEATS)
        for k in range(3):
            ag_start(ss, 1, k, 0)
        for stage in (1, 2):
            for k in range(3):
                ag_recv_wait(ss, 1, k, stage - 1)
                ag_start(ss, 1, k, stage)

    for k in range(3):
        ag_recv_wait(ss, 1, k, 2)
        gathered_out[3 + k].start()
        grad_sum = None
        for q in range(RING):
            part = contract_last(rows_of(ss, k, q), wd[:, columns(k, q)])
            grad_sum = part if grad_sum is None else grad_sum + part
        if k == 0:
            acc[2] = grad_sum
        else:
            acc[2] += grad_sum

    gate_pre = acc[0]
    up_value = acc[1]
    hidden_grad = acc[2]
    sigma = jax.nn.sigmoid(gate_pre)
    activated = gate_pre * sigma
    slope = sigma * (1.0 + gate_pre * (1.0 - sigma))
    hidden = (activated * up_value).astype(BF16)
    hid_o[...] = hidden
    row_part = jnp.sum(hidden_grad * hidden.astype(F32), axis=1, keepdims=True)
    gg_o[...] = (hidden_grad * up_value * slope).astype(BF16)
    ug_o[...] = (hidden_grad * activated).astype(BF16)
    extra = g2[0, :, :, :, FEATS[2] :].reshape(quartets * ROWS, EXTRA).astype(F32)
    weight = row_part * jnp.sum(extra, axis=1, keepdims=True)
    row_hi, row_lo = hi_lo(row_part)
    lane = lax.broadcasted_iota(jnp.int32, (quartets * ROWS, EXTRA), 1)
    row_lanes = jnp.where(lane == 0, row_hi, jnp.where(lane == 1, row_lo, 0.0)).astype(BF16)

    def rs_copies(k, stage):
        order = ORDERS[k]
        dim = order[stage]
        src = (rs, a0, a1)[stage][k]
        dst = (rb0, rb1, rb2)[stage][k]
        left = [d for d in range(3) if d not in order[:stage]]
        copies = []
        for off in OFFS:
            index = tuple(ring_index(d, off) if d == dim else slice(None) for d in left)
            copies.append(
                remote(
                    src.at[index], dst.at[off - 1],
                    rs_send.at[k, stage, off], rs_recv.at[k, stage, off], peer(dim, off),
                )
            )
        return copies

    def rs_start(k, stage):
        for copy in rs_copies(k, stage):
            copy.start()

    def rs_sum(k, stage):
        for copy in rs_copies(k, stage):
            copy.wait_recv()
        order = ORDERS[k]
        dim = order[stage]
        src = (rs, a0, a1)[stage][k]
        got = (rb0, rb1, rb2)[stage][k]
        left = [d for d in range(3) if d not in order[:stage]]
        index = tuple(at[d] if d == dim else slice(None) for d in left)
        return (src[index].astype(F32) + got[0].astype(F32)) + (
            got[1].astype(F32) + got[2].astype(F32)
        )

    srb[0, yy] = jnp.zeros((2 * RING, QUARTER + EXTRA), F32)
    gg = gg_o[...]
    ug = ug_o[...]
    for k in range(3):
        for q in range(RING):
            part = jnp.dot(gg, wg[:, columns(k, q)], preferred_element_type=F32) + jnp.dot(
                ug, wu[:, columns(k, q)], preferred_element_type=F32
            )
            shape = (RING, RING, ROWS, FEATS[k])
            rs[k][q, :, :, :, : FEATS[k]] = part.astype(BF16).reshape(shape)
            if k == 2:
                rs[k][q, :, :, :, FEATS[k] :] = row_lanes.reshape(RING, RING, ROWS, EXTRA)
            rows = rows_of(gs, k, q).astype(F32)
            cols = slice(STARTS[k], STARTS[k] + FEATS[k])
            srb[0, yy, 2 * q : 2 * q + 1, cols] = jnp.sum(part * rows, axis=0, keepdims=True)
            srb[0, yy, 2 * q + 1 : 2 * q + 2, cols] = jnp.sum(
                weight * rows, axis=0, keepdims=True
            )
        rs_start(k, 0)

    def st_copies(stage):
        here = srb.at[stage, at[stage]]
        return [
            remote(
                here, here, st_send.at[stage, off], st_recv.at[stage, off], peer(stage, off)
            )
            for off in OFFS
        ]

    def st_sum(stage):
        for copy in st_copies(stage):
            copy.wait()
        return (srb[stage, 0] + srb[stage, 1]) + (srb[stage, 2] + srb[stage, 3])

    for copy in st_copies(0):
        copy.start()
    for stage in (0, 1):
        for k in range(3):
            (a0, a1)[stage][k][...] = rs_sum(k, stage)
            rs_start(k, stage + 1)
        srb[stage + 1, at[stage + 1]] = st_sum(stage)
        for copy in st_copies(stage + 1):
            copy.start()
    for k in range(3):
        u[yy, 0:ROWS, STARTS[k] : STARTS[k] + WIDTHS[k]] = rs_sum(k, 2)

    def back_copies():
        return [
            remote(
                u.at[yy, pl.ds(0, ROWS)], u.at[yy, pl.ds(0, ROWS)],
                un_send.at[off], un_recv.at[off], peer(0, off),
            )
            for off in OFFS
        ]

    def back_over_copy(q):
        return remote(
            u.at[yy, pl.ds(0, 8)], u.at[yy, pl.ds(ROWS, 8)],
            un_send.at[0], un_recv.at[RING + q], same_pipe(prev_last),
        )

    def back_over_wait(q):
        return remote(
            u.at[q, pl.ds(0, 8)], u.at[q, pl.ds(ROWS, 8)],
            un_send.at[0], un_recv.at[RING + q], same_pipe(prev_last),
        )

    for copy in back_copies():
        copy.start()
    back_over_copy(yy).start()
    for copy in back_copies():
        copy.wait_recv()

    @pl.when(yy == RING - 1)
    def _():
        for q in range(RING):
            back_over_wait(q).wait_recv()

    first = pl.multiple_of(lax.div(yy, 2) * 8, 8)
    odd = lax.rem(yy, 2) == 1

    def owned(q, cols):
        a = u[q, pl.ds(first, 8), cols]
        b = u[q, pl.ds(first + 8, 8), cols]
        low = lax.broadcasted_iota(jnp.int32, a.shape, 0) < BLOCK
        turned = jnp.where(low, pltpu.roll(a, BLOCK, 0), pltpu.roll(b, BLOCK, 0))
        return jnp.where(odd, turned, a)

    feats = slice(0, QUARTER)
    total = jnp.zeros((2 * BLOCK, 1), F32)
    for q in range(RING):
        hat_grad = owned(q, feats) * gain_in[q]
        total = total + jnp.sum(hat_grad * hat_in[q], axis=1, keepdims=True)
    mean = total / float(RING * QUARTER)
    row_sum = jnp.sum(owned(0, slice(QUARTER, QUARTER + EXTRA)), axis=1, keepdims=True)
    logit_grad = row_sum * sc[2][:, 0:1]
    inverse = sc[3][:, 0:1]
    for q in range(RING):
        hat_grad = owned(q, feats) * gain_in[q]
        delta = inverse * (hat_grad - hat_in[q] * mean) + logit_grad * wr_in[q]
        fresh = (up_ref[q] + delta).astype(BF16)
        nbsend[q, :, :QUARTER] = fresh
        nbsend[q, :, QUARTER:] = sc[4].astype(BF16)
        new_o[q] = fresh

    @pl.when(pipe == 1)
    def _():
        nb_copy().start()
        nb_o[...] = nbsend[...]

    @pl.when(pipe == 0)
    def _():
        nb_o[...] = nb[...]

    st_o[...] = st_sum(2)

    ag_send_wait(gs, 0)
    ag_send_wait(ss, 1)
    for k in range(3):
        for stage in range(3):
            for copy in rs_copies(k, stage):
                copy.wait_send()
    for copy in back_copies():
        copy.wait_send()
    back_over_copy(yy).wait_send()

    @pl.when(pipe == 1)
    def _():
        nb_copy().wait_send()

    for copy in gathered_out:
        copy.wait()


def communicate(bn, up, hat, gain, wr, sc, wg, wu, wd):
    ff = wg.shape[0]
    rows = RING * RING * ROWS
    width = QUARTER + EXTRA
    vmem = pl.BlockSpec(memory_space=pltpu.VMEM)
    hbm = pl.BlockSpec(memory_space=pl.ANY)
    cube = (RING, RING, RING, ROWS)
    shape = jax.ShapeDtypeStruct
    out_shape = (
        [shape(cube + (w,), BF16) for w in WIDTHS]
        + [shape(cube + (w,), BF16) for w in FEATS]
        + [shape((rows, ff), BF16)] * 3
        + [shape((RING, 8, width), BF16), shape((RING, 8, QUARTER), BF16)]
        + [shape((8, width), F32)]
    )
    dma = pltpu.SemaphoreType.DMA
    scratch = (
        [pltpu.VMEM((RING, 8, QUARTER), F32), pltpu.VMEM((RING, 8, QUARTER), BF16)]
        + [pltpu.VMEM((5, 8, width), BF16), pltpu.VMEM((5, 8, QUARTER), BF16)]
        + [pltpu.VMEM(cube + (w,), BF16) for w in WIDTHS]
        + [pltpu.VMEM(cube + (w,), BF16) for w in FEATS]
        + [pltpu.VMEM(cube + (w,), BF16) for w in WIDTHS]
        + [pltpu.VMEM((3, RING, RING, ROWS, w), BF16) for w in WIDTHS]
        + [pltpu.VMEM((RING, RING, ROWS, w), F32) for w in WIDTHS]
        + [pltpu.VMEM((3, RING, ROWS, w), F32) for w in WIDTHS]
        + [pltpu.VMEM((RING, ROWS, w), F32) for w in WIDTHS]
        + [pltpu.VMEM((3, ROWS, w), F32) for w in WIDTHS]
        + [pltpu.VMEM((RING, ROWS + 8, width), F32)]
        + [pltpu.VMEM((RING, 8, width), BF16)] * 2
        + [pltpu.VMEM((3, RING, 8, width), F32)]
        + [pltpu.VMEM((3, rows, ff), F32)]
        + [pltpu.VMEM(wg.shape, BF16)] * 3
        + [dma((2, 8)), dma((2, 4))]
        + [dma((2, 3, 3, 4)), dma((2, 3, 3, 4))]
        + [dma((3, 3, 4)), dma((3, 3, 4))]
        + [dma((3, 4)), dma((3, 4))]
        + [dma((4,)), dma((8,))]
        + [dma, dma]
        + [dma((9,))]
    )
    return pl.pallas_call(
        step_kernel,
        out_shape=out_shape,
        in_specs=[vmem] * 6 + [hbm] * 3,
        out_specs=[hbm] * 6 + [vmem] * 6,
        scratch_shapes=scratch,
        compiler_params=pltpu.CompilerParams(
            collective_id=0, has_side_effects=True, vmem_limit_bytes=56 * 1024 * 1024
        ),
        name="routed_step",
    )(bn, up, hat, gain, wr, sc, wg, wu, wd)


def weight_kernel(hid, gg, ug, g0, g1, g2, s0, s1, s2, out_gate, out_up, out_down):
    rows = hid.shape[0]
    for k, (g, s) in enumerate(zip((g0, g1, g2), (s0, s1, s2))):
        cols = slice(STARTS[k], STARTS[k] + FEATS[k])
        normed = g[0, :, :, :, : FEATS[k]].reshape(rows, FEATS[k])
        scaled = s[0].reshape(rows, FEATS[k])
        out_gate[:, cols] = contract_first(gg[...], normed)
        out_up[:, cols] = contract_first(ug[...], normed)
        out_down[:, cols] = contract_first(hid[...], scaled)


def weight_grads(hid, gg, ug, gathered, ff, model_dim):
    small = pl.BlockSpec(hid.shape, lambda q: (0, 0))

    def part(width):
        return pl.BlockSpec((1, RING, RING, ROWS, width), lambda q: (q, 0, 0, 0, 0))

    out = pl.BlockSpec((ff, QUARTER), lambda q: (0, q))
    return pl.pallas_call(
        weight_kernel,
        grid=(RING,),
        out_shape=[jax.ShapeDtypeStruct((ff, model_dim), F32)] * 3,
        in_specs=[small] * 3 + [part(w) for w in WIDTHS + FEATS],
        out_specs=[out] * 3,
        compiler_params=pltpu.CompilerParams(vmem_limit_bytes=40 * 1024 * 1024),
        name="weight_grads",
    )(hid, gg, ug, *gathered)


def quarters(rows):
    count = rows.shape[0]
    return rows.reshape(count, RING, QUARTER).transpose(1, 0, 2)


def on_device(saved, grad_out, route_blocks, route_dest, gain, w_router, w_gate, w_up, w_down):
    me = lax.axis_index("ctx")
    tokens = saved[0]
    tok_rows, model_dim = tokens.shape
    block_count = tok_rows // BLOCK
    blocks = route_blocks[0, 0]
    targets = route_dest[0, 0]
    kept = targets[0] == me
    keep_block = jnp.where(kept, blocks[0], blocks[1])
    hand_block = jnp.where(kept, blocks[1], blocks[0])
    handed = jnp.where(kept, targets[1] >= 0, targets[0] >= 0)

    def pick(array):
        by_block = array.reshape(block_count, BLOCK, model_dim)
        return jnp.concatenate(
            [
                lax.dynamic_index_in_dim(by_block, keep_block, 0, keepdims=False),
                lax.dynamic_index_in_dim(by_block, hand_block, 0, keepdims=False),
            ],
            axis=0,
        )

    first = jnp.arange(2 * BLOCK)[:, None] < BLOCK
    mask = jnp.where(first, kept, handed).astype(F32)
    block_id = jnp.where(first, keep_block, hand_block).astype(F32)
    gain_row = gain[0]
    router_row = w_router[0].astype(F32)
    picked = pick(tokens).astype(F32)
    inverse = lax.rsqrt(jnp.mean(picked * picked, axis=1, keepdims=True) + EPSILON)
    hat = picked * inverse
    router = jax.nn.sigmoid(jnp.sum(picked * router_row, axis=1, keepdims=True))
    normed = (hat * gain_row * mask).astype(BF16)
    carried = (1.0 - router) * mask / inverse
    carried_hi = lax.reduce_precision(carried, 8, 7)
    carried_lo = carried - carried_hi
    lane = jnp.arange(EXTRA)[None, :]
    extra = jnp.where(lane == 0, carried_hi, jnp.where(lane == 1, carried_lo, 0.0)).astype(BF16)
    bn = jnp.concatenate(
        [quarters(normed), jnp.broadcast_to(extra[None], (RING,) + extra.shape)], axis=2
    )
    scalars = jnp.stack(
        [inverse, router * mask, (1.0 - router) * mask, inverse * mask, block_id]
    )
    scalars = jnp.broadcast_to(scalars, scalars.shape[:2] + (EXTRA,))
    upstream = quarters(pick(grad_out).astype(F32))
    results = communicate(
        bn,
        upstream,
        quarters(hat),
        quarters(gain_row[None]),
        quarters(router_row[None]),
        scalars,
        w_gate[0],
        w_up[0],
        w_down[0],
    )
    gathered = results[:6]
    hid, gg, ug, nb, fresh, stats = results[6:]
    grads = weight_grads(hid, gg, ug, gathered, w_gate.shape[1], model_dim)

    def whole(rows):
        return rows[:, :, :QUARTER].transpose(1, 0, 2).reshape(2, BLOCK, model_dim)

    above = whole(nb)
    above_ids = nb[0, :: BLOCK, QUARTER].astype(jnp.int32)
    own = whole(fresh)
    ids = jnp.arange(block_count, dtype=jnp.int32)[:, None, None]
    outcome = grad_out.reshape(block_count, BLOCK, model_dim)
    for rows, where in (
        (above[0], above_ids[0]),
        (above[1], above_ids[1]),
        (own[0], keep_block),
        (own[1], hand_block),
    ):
        outcome = jnp.where(ids == where, rows[None], outcome)
    by_row = stats[:, :QUARTER].reshape(RING, 2, QUARTER)
    stat_gain = by_row[:, 0].reshape(model_dim) / gain_row
    stat_router = by_row[:, 1].reshape(model_dim) / gain_row
    return (
        outcome.reshape(tok_rows, model_dim)[None],
        grads[0][None],
        grads[1][None],
        grads[2][None],
        stat_gain[None],
        stat_router[None],
    )


def solution(mesh):
    in_specs = (
        P("pipe", "ctx", None),
        P("ctx", None),
        P("pipe", "ctx", None),
        P("pipe", "ctx", None),
        P("pipe", None),
        P("pipe", None),
        P("pipe", "ctx", None),
        P("pipe", "ctx", None),
        P("pipe", "ctx", None),
    )
    out_specs = (
        P("pipe", "ctx", None),
        P("pipe", "ctx", None),
        P("pipe", "ctx", None),
        P("pipe", "ctx", None),
        P("pipe", None),
        P("pipe", None),
    )
    return jax.shard_map(
        on_device, mesh=mesh, in_specs=in_specs, out_specs=out_specs, check_vma=False
    )
```

time: 1360 us -> 149 us (0.11)
  blocking collectives: 692 us -> 0 us
  waiting for transfers between devices: 552 us -> 0 us
  Pallas kernels: 0 us -> 111 us
  matrix products: 54.3 us -> 0 us
  other arithmetic: 23.2 us -> 8.29 us
    reduce_scatter x2 -> x0, waiting for transfers between devices: 350 us -> none  [on_device(): lax.psum_scatter(grads_all, 'ctx', scatter_dimension=0, tiled=True)]
    unnamed x2 -> x0, blocking collectives: 350 us -> none
    psum x1 -> x0, blocking collectives: 342 us -> none  [on_device(): gain_part, router_part = lax.psum((gain_part, router_part), 'ctx')]
    all_gather x3 -> x0, waiting for transfers between devices: 198 us -> none  [the longest x2 126 us: on_device(): lax.all_gather(scaled.reshape(slot_count * BLOCK, model_dim), 'ctx', axis...]
    pallas_call x0 -> x2, Pallas kernels: none -> 111 us  [the longest x1 106 us: communicate(): pl.pallas_call(step_kernel, out_shape=out_shape, in_specs=[vmem] * 6 + [h...]
    dot_general x15 -> x0, matrix products: 54.3 us -> none  [the longest x6 23.9 us: contract_first(): lax.dot_general(left_side, right_side, (((0,), (0,)), ((), ())), preferre...]
  transfers between devices with their start and end apart: 6 -> 0, of which waited for: 6 -> 0; matrix products, arithmetic and copies ran while one was open for 3% -> 0% of each run, Pallas kernels for 0% -> 0%
where the time goes in v1:
time: 149 us; the launch traced here: 148 us
  Pallas kernels  111 us (74%)
  local copies, waits for them, and re-layouts  23.2 us (16%)
  other arithmetic  8.29 us (6%)
  between operations  5.47 us (4%)
    pallas_call x1, Pallas kernels, communicate(): pl.pallas_call(step_kernel, out_shape=out_shape, in_specs=[vmem] * 6 + [h...  106 us
    unnamed x36, local copies, waits for them, and re-layouts  9.96 us
    broadcast_in_dim x16, local copies, waits for them, and re-layouts, on_device(): outcome = jnp.where(ids == where, rows[None], outcome)  6.24 us
    pallas_call x1, Pallas kernels, weight_grads(): pl.pallas_call(weight_kernel, grid=(RING,), out_shape=[jax.ShapeDtypeStru...  5.1 us
    select_n x1, other arithmetic, on_device(): outcome = jnp.where(ids == where, rows[None], outcome)  3.19 us

profile of v1, /device:TPU:0, one launch (start us, length us, event | category | flops | bytes accessed | tf_op | source)
XLA Modules:
  0.0 147.7 jit_solution(13831907810456979120)
XLA Ops:
  0.7 1.3 fusion.14
  2.6 1.3 fusion.15
  6.5 1.5 reshape.335
  8.0 1.5 reshape_squeeze.9
  11.2 0.7 broadcast_in_dim.180.sc
  11.9 0.7 convert_bitcast_fusion.up_in
  13.1 0.7 reduce.3
  13.8 0.7 fusion.2
  15.3 105.7 %routed_step.1 = (bf16[4,4,4,16,384]{4,3,2,1,0:T(8,128)(2,1)}, bf16[4,4,4,16,384]{4,3,2,1,0:T(8,128)(2,1)}, bf16[4,4,4,16,384]{4,3,2,1,0:T(8,128)(2,1)}, bf16[4,...) custom-call(bf16[4,8,1152]{2,1,0:T(8,128)(2,1)} %pad_maximum_fusion., ...), custom_call_target="tpu_custom_call" | custom-call | tf_op jit(solution)/shard_map/routed_step/pallas_call | solution.py:518
  121.0 1.1 copy-done
  122.1 1.1 copy-done.1
  123.3 1.1 copy-done.2
  124.4 1.1 copy-done.3
  125.5 1.1 copy-done.4
  126.7 1.0 copy-done.5
  127.7 0.9 copy-done.6
  128.6 0.9 copy-done.7
  129.5 0.9 copy-done.8
  130.4 5.1 %weight_grads.1 = (f32[224,4096]{1,0:T(8,128)}, f32[224,4096]{1,0:T(8,128)}, f32[224,4096]{1,0:T(8,128)}) custom-call(bf16[256,224]{1,0:T(8,128)(2,1)S(1)} %copy-done.6, bf16[256,224]{1,0:T(8,128)(2,1)S(1)} %copy-done.7, bf16[256,224]{1,0:T(8,128)(2,1)S(1)} %copy-done.8, bf16[4,4,4,16,384]{4,3,2,1,0:T(8,128)(2,1)S(1)} %copy-done, ...), custom_call_target="tpu_custom_call" | custom-call | tf_op jit(solution)/shard_map/weight_grads/pallas_call | solution.py:549
  136.8 1.1 broadcast_in_dim.201
  138.4 1.1 broadcast_in_dim.183
  140.0 1.1 broadcast_in_dim.189
  142.5 0.7 iota_compare_fusion
  143.8 3.2 %select_bitcast_fusion = bf16[1,128,4096]{2,1,0:T(8,128)(2,1)} fusion(bf16[128,4096]{1,0:T(8,128)(2,1)} %broadcast_in_dim.183, bf16[128,4096]{1,0:T(8,128)(2,1)} %broadcast_in_dim.189, bf16[128,4096]{1,0:T(8,128)(2,1)S(1)} %broadcast_in_dim.195, bf16[128,4096]{1,0:T(8,128)(2,1)} %broadcast_in_dim.201, bf16[128,4096]{1,0:T(8,128)(2,1)S(1)} %copy-done.9, ...), kind=kLoop, calls=%fused_computation | loop fusion | flops 2097152 | bytes 6291968 | tf_op jit(solution)/shard_map/jit(_where)/select_n | solution.py:639
  (70 shorter events, 6.5 us)
Async XLA Ops:
  0.6 8.9 %copy-start.16 = (bf16[1,4096]{1,0:T(2,128)(2,1)S(1)}, bf16[1,4096]{1,0:T(2,128)(2,1)}, u32[]{:S(2)}) copy-start(bf16[1,4096]{1,0:T(2,128)(2,1)} %param.14) | copy-start | bytes 24580
  0.6 12.4 %copy-start.10 = (f32[1,4096]{1,0:T(1,128)S(1)}, f32[1,4096]{1,0:T(1,128)}, u32[]{:S(2)}) copy-start(f32[1,4096]{1,0:T(1,128)} %param.13) | copy-start | bytes 49156
  9.6 5.7 %copy-start.12 = (f32[1,4096]{1,0:T(1,128)}, f32[1,4096]{1,0:T(1,128)S(1)}, u32[]{:S(2)}) copy-start(f32[1,4096]{1,0:T(1,128)S(1)} %mul.74) | copy-start | bytes 49156
  121.0 1.1 copy-start
  122.1 1.1 copy-start.1
  123.3 1.1 copy-start.2
  124.4 1.1 copy-start.3
  125.5 1.1 copy-start.4
  126.7 1.0 copy-start.5
  127.7 0.9 copy-start.6
  128.6 0.9 copy-start.7
  129.5 0.9 copy-start.8
  130.4 5.1 %copy-start.14 = (bf16[4,8,1152]{2,1,0:T(8,128)(2,1)S(1)}, bf16[4,8,1152]{2,1,0:T(8,128)(2,1)}, u32[]{:S(2)}) copy-start(bf16[4,8,1152]{2,1,0:T(8,128)(2,1)} %get-tuple-element.22) | copy-start | bytes 221188
  135.5 2.4 %copy-start.13 = (bf16[4,8,1024]{2,1,0:T(8,128)(2,1)S(1)}, bf16[4,8,1024]{2,1,0:T(8,128)(2,1)}, u32[]{:S(2)}) copy-start(bf16[4,8,1024]{2,1,0:T(8,128)(2,1)} %get-tuple-element.21) | copy-start | bytes 196612
  137.9 5.9 %copy-start.9 = (bf16[128,4096]{1,0:T(8,128)(2,1)S(1)}, bf16[128,4096]{1,0:T(8,128)(2,1)}, u32[]{:S(2)}) copy-start(bf16[128,4096]{1,0:T(8,128)(2,1)} %param.10) | copy-start | bytes 3145732
  141.1 5.9 %copy-start.15 = (f32[8,1152]{1,0:T(8,128)S(1)}, f32[8,1152]{1,0:T(8,128)}, u32[]{:S(2)}) copy-start(f32[8,1152]{1,0:T(8,128)} %get-tuple-element.35) | copy-start | bytes 110596
  141.1 5.9 %copy-start.11 = (f32[1,4096]{1,0:T(1,128)S(1)}, f32[1,4096]{1,0:T(1,128)}, u32[]{:S(2)}) copy-start(f32[1,4096]{1,0:T(1,128)} %param.13) | copy-start | bytes 49156

commit v2 on v1

--- a/solution.py
+++ b/solution.py
@@ -39,11 +39,12 @@
 
 
 def step_kernel(
-    bn, up_in, hat_in, gain_in, wr_in, sc, wg_hbm, wu_hbm, wd_hbm,
+    blocks, targets, saved_hbm, grad_hbm, gain_hbm, router_hbm, wg_hbm, wu_hbm, wd_hbm,
     go0, go1, go2, so0, so1, so2, hid_o, gg_o, ug_o, nb_o, new_o, st_o,
-    up_ref, bs, hn, hs, g0, g1, g2, s0, s1, s2, r0, r1, r2,
+    saved, grad_out, gain, router_row, hat_ref, up_ref, sc, bn,
+    bs, hn, hs, g0, g1, g2, s0, s1, s2, r0, r1, r2,
     rb00, rb01, rb02, a00, a01, a02, rb10, rb11, rb12, a10, a11, a12, rb20, rb21, rb22,
-    u, nb, nbsend, srb, acc, wg, wu, wd,
+    u, nb, srb, acc, wg, wu, wd,
     hand_send, hand_recv, ag_send, ag_recv, rs_send, rs_recv, st_send, st_recv,
     un_send, un_recv, nb_send, nb_recv, local_sem,
 ):
@@ -82,11 +83,22 @@
     rb1, a1 = (rb10, rb11, rb12), (a10, a11, a12)
     rb2 = (rb20, rb21, rb22)
 
+    row_copies = [
+        pltpu.make_async_copy(src, dst, local_sem.at[9 + i])
+        for i, (src, dst) in enumerate(
+            (
+                (saved_hbm.at[0], saved),
+                (gain_hbm, gain),
+                (router_hbm, router_row),
+                (grad_hbm, grad_out),
+            )
+        )
+    ]
     weight_copies = [
-        pltpu.make_async_copy(src, dst, local_sem.at[i])
+        pltpu.make_async_copy(src.at[0], dst, local_sem.at[i])
         for i, (src, dst) in enumerate(((wg_hbm, wg), (wu_hbm, wu), (wd_hbm, wd)))
     ]
-    for copy in weight_copies:
+    for copy in row_copies + weight_copies:
         copy.start()
 
     barrier = pltpu.get_barrier_semaphore()
@@ -104,6 +116,52 @@
     def _():
         for j in range(RING):
             greet(same_pipe(next_base + j))
+
+    kept = targets[0, 0, 0] == me
+    keep_block = jnp.where(kept, blocks[0, 0, 0], blocks[0, 0, 1])
+    hand_block = jnp.where(kept, blocks[0, 0, 1], blocks[0, 0, 0])
+    handed = jnp.where(kept, targets[0, 0, 1], targets[0, 0, 0]) >= 0
+    first_rows = lax.broadcasted_iota(jnp.int32, (2 * BLOCK, 1), 0) < BLOCK
+    mask = jnp.where(
+        first_rows, jnp.where(kept, 1.0, 0.0).astype(F32), jnp.where(handed, 1.0, 0.0).astype(F32)
+    )
+
+    block_id = jnp.where(first_rows, keep_block, hand_block)
+    row_in_block = lax.rem(lax.broadcasted_iota(jnp.int32, (2 * BLOCK, 1), 0), BLOCK)
+    tokens = lax.broadcasted_iota(jnp.int32, (2 * BLOCK, saved.shape[0]), 1)
+    chosen = jnp.where(tokens == block_id * BLOCK + row_in_block, 1.0, 0.0).astype(BF16)
+
+    def pick(array, cols):
+        return jnp.dot(chosen, array[:, cols], preferred_element_type=F32)
+
+    def quarter(q):
+        return slice(q * QUARTER, (q + 1) * QUARTER)
+
+    for copy in row_copies[:3]:
+        copy.wait()
+    squares = jnp.zeros((2 * BLOCK, 1), F32)
+    logits = jnp.zeros((2 * BLOCK, 1), F32)
+    for q in range(RING):
+        rows = pick(saved, quarter(q))
+        hat_ref[q] = rows
+        squares += jnp.sum(rows * rows, axis=1, keepdims=True)
+        logits += jnp.sum(rows * router_row[:, quarter(q)].astype(F32), axis=1, keepdims=True)
+    inverse = lax.rsqrt(squares / float(RING * QUARTER) + EPSILON)
+    router = jax.nn.sigmoid(logits)
+    rest = (1.0 - router) * mask
+    carried_hi, carried_lo = hi_lo(rest / inverse)
+    lane = lax.broadcasted_iota(jnp.int32, (2 * BLOCK, EXTRA), 1)
+    extra = jnp.where(lane == 0, carried_hi, jnp.where(lane == 1, carried_lo, 0.0)).astype(BF16)
+    for q in range(RING):
+        hat = hat_ref[q] * inverse
+        hat_ref[q] = hat
+        bn[q, :, :QUARTER] = (hat * gain[:, quarter(q)] * mask).astype(BF16)
+        bn[q, :, QUARTER:] = extra
+    for i, value in enumerate((router * mask, rest, inverse * mask, block_id.astype(F32))):
+        sc[i] = jnp.broadcast_to(value, (2 * BLOCK, EXTRA))
+    row_copies[3].wait()
+    for q in range(RING):
+        up_ref[q] = pick(grad_out, quarter(q))
 
     pl.semaphore_wait(barrier, 11 + RING * lax.div(yy, RING - 1))
 
@@ -183,11 +241,10 @@
 
     def make_scaled():
         for q in range(RING):
-            bs[q] = (sc[1][:, 0:1] * up_ref[q]).astype(BF16)
+            bs[q] = (sc[0][:, 0:1] * up_ref[q]).astype(BF16)
 
     @pl.when(pipe == 1)
     def _():
-        up_ref[...] = up_in[...]
         make_scaled()
 
     hand_start(bn, hn, 0)
@@ -252,20 +309,20 @@
             acc[1] += up_sum
 
     def nb_copy():
-        return remote(nbsend, nb, nb_send, nb_recv, partner)
+        return remote(new_o, nb, nb_send, nb_recv, partner)
 
     @pl.when(pipe == 0)
     def _():
         nb_copy().wait_recv()
         low = lax.broadcasted_iota(jnp.int32, (2 * BLOCK, 1), 0) < BLOCK
-        mine = sc[4][:, 0:1]
+        mine = sc[3][:, 0:1]
         same = 1.0 - jnp.minimum(jnp.abs(nb[0, :, QUARTER : QUARTER + 1].astype(F32) - mine), 1.0)
         other = pltpu.roll(nb[0, :, QUARTER:].astype(F32), BLOCK, 0)[:, 0:1]
         cross = 1.0 - jnp.minimum(jnp.abs(other - mine), 1.0)
         for q in range(RING):
             rows = nb[q, :, :QUARTER].astype(F32)
             turned = pltpu.roll(rows, BLOCK, 0)
-            kept_rows = (1.0 - same - cross) * up_in[q]
+            kept_rows = (1.0 - same - cross) * up_ref[q]
             up_ref[q] = same * rows + cross * turned + kept_rows
         make_scaled()
         hand_start(bs, hs, 1)
@@ -432,24 +489,24 @@
     feats = slice(0, QUARTER)
     total = jnp.zeros((2 * BLOCK, 1), F32)
     for q in range(RING):
-        hat_grad = owned(q, feats) * gain_in[q]
-        total = total + jnp.sum(hat_grad * hat_in[q], axis=1, keepdims=True)
+        hat_grad = owned(q, feats) * gain[:, quarter(q)]
+        total = total + jnp.sum(hat_grad * hat_ref[q], axis=1, keepdims=True)
     mean = total / float(RING * QUARTER)
     row_sum = jnp.sum(owned(0, slice(QUARTER, QUARTER + EXTRA)), axis=1, keepdims=True)
-    logit_grad = row_sum * sc[2][:, 0:1]
-    inverse = sc[3][:, 0:1]
+    logit_grad = row_sum * sc[1][:, 0:1]
+    scale = sc[2][:, 0:1]
     for q in range(RING):
-        hat_grad = owned(q, feats) * gain_in[q]
-        delta = inverse * (hat_grad - hat_in[q] * mean) + logit_grad * wr_in[q]
-        fresh = (up_ref[q] + delta).astype(BF16)
-        nbsend[q, :, :QUARTER] = fresh
-        nbsend[q, :, QUARTER:] = sc[4].astype(BF16)
-        new_o[q] = fresh
+        hat_grad = owned(q, feats) * gain[:, quarter(q)]
+        delta = scale * (hat_grad - hat_ref[q] * mean) + logit_grad * router_row[
+            :, quarter(q)
+        ].astype(F32)
+        new_o[q, :, :QUARTER] = (up_ref[q] + delta).astype(BF16)
+        new_o[q, :, QUARTER:] = sc[3].astype(BF16)
 
     @pl.when(pipe == 1)
     def _():
         nb_copy().start()
-        nb_o[...] = nbsend[...]
+        nb_o[...] = new_o[...]
 
     @pl.when(pipe == 0)
     def _():
@@ -475,11 +532,12 @@
         copy.wait()
 
 
-def communicate(bn, up, hat, gain, wr, sc, wg, wu, wd):
-    ff = wg.shape[0]
+def communicate(route_blocks, route_dest, saved, grad_out, gain, w_router, wg, wu, wd):
+    ff = wg.shape[1]
     rows = RING * RING * ROWS
     width = QUARTER + EXTRA
     vmem = pl.BlockSpec(memory_space=pltpu.VMEM)
+    smem = pl.BlockSpec(memory_space=pltpu.SMEM)
     hbm = pl.BlockSpec(memory_space=pl.ANY)
     cube = (RING, RING, RING, ROWS)
     shape = jax.ShapeDtypeStruct
@@ -487,12 +545,16 @@
         [shape(cube + (w,), BF16) for w in WIDTHS]
         + [shape(cube + (w,), BF16) for w in FEATS]
         + [shape((rows, ff), BF16)] * 3
-        + [shape((RING, 8, width), BF16), shape((RING, 8, QUARTER), BF16)]
+        + [shape((RING, 8, width), BF16)] * 2
         + [shape((8, width), F32)]
     )
     dma = pltpu.SemaphoreType.DMA
     scratch = (
-        [pltpu.VMEM((RING, 8, QUARTER), F32), pltpu.VMEM((RING, 8, QUARTER), BF16)]
+        [pltpu.VMEM(grad_out.shape, BF16)] * 2
+        + [pltpu.VMEM(gain.shape, F32), pltpu.VMEM(w_router.shape, BF16)]
+        + [pltpu.VMEM((RING, 8, QUARTER), F32)] * 2
+        + [pltpu.VMEM((4, 8, EXTRA), F32), pltpu.VMEM((RING, 8, width), BF16)]
+        + [pltpu.VMEM((RING, 8, QUARTER), BF16)]
         + [pltpu.VMEM((5, 8, width), BF16), pltpu.VMEM((5, 8, QUARTER), BF16)]
         + [pltpu.VMEM(cube + (w,), BF16) for w in WIDTHS]
         + [pltpu.VMEM(cube + (w,), BF16) for w in FEATS]
@@ -503,151 +565,101 @@
         + [pltpu.VMEM((RING, ROWS, w), F32) for w in WIDTHS]
         + [pltpu.VMEM((3, ROWS, w), F32) for w in WIDTHS]
         + [pltpu.VMEM((RING, ROWS + 8, width), F32)]
-        + [pltpu.VMEM((RING, 8, width), BF16)] * 2
+        + [pltpu.VMEM((RING, 8, width), BF16)]
         + [pltpu.VMEM((3, RING, 8, width), F32)]
         + [pltpu.VMEM((3, rows, ff), F32)]
-        + [pltpu.VMEM(wg.shape, BF16)] * 3
+        + [pltpu.VMEM(wg.shape[1:], BF16)] * 3
         + [dma((2, 8)), dma((2, 4))]
         + [dma((2, 3, 3, 4)), dma((2, 3, 3, 4))]
         + [dma((3, 3, 4)), dma((3, 3, 4))]
         + [dma((3, 4)), dma((3, 4))]
         + [dma((4,)), dma((8,))]
         + [dma, dma]
-        + [dma((9,))]
+        + [dma((13,))]
     )
     return pl.pallas_call(
         step_kernel,
         out_shape=out_shape,
-        in_specs=[vmem] * 6 + [hbm] * 3,
+        in_specs=[smem] * 2 + [hbm] * 7,
         out_specs=[hbm] * 6 + [vmem] * 6,
         scratch_shapes=scratch,
         compiler_params=pltpu.CompilerParams(
-            collective_id=0, has_side_effects=True, vmem_limit_bytes=56 * 1024 * 1024
+            collective_id=0, has_side_effects=True, vmem_limit_bytes=58 * 1024 * 1024
         ),
         name="routed_step",
-    )(bn, up, hat, gain, wr, sc, wg, wu, wd)
-
-
-def weight_kernel(hid, gg, ug, g0, g1, g2, s0, s1, s2, out_gate, out_up, out_down):
+    )(route_blocks, route_dest, saved, grad_out, gain, w_router, wg, wu, wd)
+
+
+def finish_kernel(
+    hid, gg, ug, g0, g1, g2, s0, s1, s2, grad_out, nb, fresh, stats, gain,
+    out_inputs, out_gate, out_up, out_down, out_gain, out_router,
+):
     rows = hid.shape[0]
     for k, (g, s) in enumerate(zip((g0, g1, g2), (s0, s1, s2))):
         cols = slice(STARTS[k], STARTS[k] + FEATS[k])
         normed = g[0, :, :, :, : FEATS[k]].reshape(rows, FEATS[k])
         scaled = s[0].reshape(rows, FEATS[k])
-        out_gate[:, cols] = contract_first(gg[...], normed)
-        out_up[:, cols] = contract_first(ug[...], normed)
-        out_down[:, cols] = contract_first(hid[...], scaled)
-
-
-def weight_grads(hid, gg, ug, gathered, ff, model_dim):
-    small = pl.BlockSpec(hid.shape, lambda q: (0, 0))
+        out_gate[0, :, cols] = contract_first(gg[...], normed)
+        out_up[0, :, cols] = contract_first(ug[...], normed)
+        out_down[0, :, cols] = contract_first(hid[...], scaled)
+    patterns = []
+    low = lax.broadcasted_iota(jnp.int32, (2 * BLOCK, QUARTER), 0) < BLOCK
+    for ref in (nb, fresh):
+        new_rows = ref[0, :, :QUARTER].astype(F32)
+        turned = pltpu.roll(new_rows, BLOCK, 0)
+        which = ref[0, :, QUARTER:].astype(F32)
+        patterns.append((which[0:1, 0:1], jnp.where(low, new_rows, turned)))
+        patterns.append((which[BLOCK : BLOCK + 1, 0:1], jnp.where(low, turned, new_rows)))
+    half = jnp.where(lax.broadcasted_iota(jnp.int32, (2 * BLOCK, 1), 0) < BLOCK, 0.0, 1.0)
+    for i in range(grad_out.shape[0] // 8):
+        block = half + float(2 * i)
+        value = grad_out[8 * i : 8 * i + 8, :].astype(F32)
+        for which, pattern in patterns:
+            value = jnp.where(block == which, pattern, value)
+        out_inputs[0, 8 * i : 8 * i + 8, :] = value.astype(BF16)
+    q = pl.program_id(0)
+    out_gain[...] = stats[pl.ds(2 * q, 1), :QUARTER] / gain[...]
+    out_router[...] = stats[pl.ds(2 * q + 1, 1), :QUARTER] / gain[...]
+
+
+def finish(hid, gg, ug, gathered, grad_out, nb, fresh, stats, gain):
+    tok_rows, model_dim = grad_out.shape
+    ff = hid.shape[1]
+
+    def whole(array):
+        return pl.BlockSpec(array.shape, lambda q: (0,) * array.ndim)
 
     def part(width):
         return pl.BlockSpec((1, RING, RING, ROWS, width), lambda q: (q, 0, 0, 0, 0))
 
-    out = pl.BlockSpec((ff, QUARTER), lambda q: (0, q))
+    new_rows = pl.BlockSpec((1,) + nb.shape[1:], lambda q: (q, 0, 0))
+    vector = pl.BlockSpec((1, QUARTER), lambda q: (0, q))
+    grads = pl.BlockSpec((1, ff, QUARTER), lambda q: (0, 0, q))
+    shape = jax.ShapeDtypeStruct
     return pl.pallas_call(
-        weight_kernel,
+        finish_kernel,
         grid=(RING,),
-        out_shape=[jax.ShapeDtypeStruct((ff, model_dim), F32)] * 3,
-        in_specs=[small] * 3 + [part(w) for w in WIDTHS + FEATS],
-        out_specs=[out] * 3,
-        compiler_params=pltpu.CompilerParams(vmem_limit_bytes=40 * 1024 * 1024),
-        name="weight_grads",
-    )(hid, gg, ug, *gathered)
-
-
-def quarters(rows):
-    count = rows.shape[0]
-    return rows.reshape(count, RING, QUARTER).transpose(1, 0, 2)
+        out_shape=[shape((1, tok_rows, model_dim), BF16)]
+        + [shape((1, ff, model_dim), F32)] * 3
+        + [shape((1, model_dim), F32)] * 2,
+        in_specs=[whole(hid)] * 3
+        + [part(w) for w in WIDTHS + FEATS]
+        + [pl.BlockSpec((tok_rows, QUARTER), lambda q: (0, q)), new_rows, new_rows]
+        + [whole(stats), vector],
+        out_specs=[pl.BlockSpec((1, tok_rows, QUARTER), lambda q: (0, 0, q))]
+        + [grads] * 3
+        + [vector] * 2,
+        compiler_params=pltpu.CompilerParams(vmem_limit_bytes=60 * 1024 * 1024),
+        name="finish",
+    )(hid, gg, ug, *gathered, grad_out, nb, fresh, stats, gain)
 
 
 def on_device(saved, grad_out, route_blocks, route_dest, gain, w_router, w_gate, w_up, w_down):
-    me = lax.axis_index("ctx")
-    tokens = saved[0]
-    tok_rows, model_dim = tokens.shape
-    block_count = tok_rows // BLOCK
-    blocks = route_blocks[0, 0]
-    targets = route_dest[0, 0]
-    kept = targets[0] == me
-    keep_block = jnp.where(kept, blocks[0], blocks[1])
-    hand_block = jnp.where(kept, blocks[1], blocks[0])
-    handed = jnp.where(kept, targets[1] >= 0, targets[0] >= 0)
-
-    def pick(array):
-        by_block = array.reshape(block_count, BLOCK, model_dim)
-        return jnp.concatenate(
-            [
-                lax.dynamic_index_in_dim(by_block, keep_block, 0, keepdims=False),
-                lax.dynamic_index_in_dim(by_block, hand_block, 0, keepdims=False),
-            ],
-            axis=0,
-        )
-
-    first = jnp.arange(2 * BLOCK)[:, None] < BLOCK
-    mask = jnp.where(first, kept, handed).astype(F32)
-    block_id = jnp.where(first, keep_block, hand_block).astype(F32)
-    gain_row = gain[0]
-    router_row = w_router[0].astype(F32)
-    picked = pick(tokens).astype(F32)
-    inverse = lax.rsqrt(jnp.mean(picked * picked, axis=1, keepdims=True) + EPSILON)
-    hat = picked * inverse
-    router = jax.nn.sigmoid(jnp.sum(picked * router_row, axis=1, keepdims=True))
-    normed = (hat * gain_row * mask).astype(BF16)
-    carried = (1.0 - router) * mask / inverse
-    carried_hi = lax.reduce_precision(carried, 8, 7)
-    carried_lo = carried - carried_hi
-    lane = jnp.arange(EXTRA)[None, :]
-    extra = jnp.where(lane == 0, carried_hi, jnp.where(lane == 1, carried_lo, 0.0)).astype(BF16)
-    bn = jnp.concatenate(
-        [quarters(normed), jnp.broadcast_to(extra[None], (RING,) + extra.shape)], axis=2
-    )
-    scalars = jnp.stack(
-        [inverse, router * mask, (1.0 - router) * mask, inverse * mask, block_id]
-    )
-    scalars = jnp.broadcast_to(scalars, scalars.shape[:2] + (EXTRA,))
-    upstream = quarters(pick(grad_out).astype(F32))
     results = communicate(
-        bn,
-        upstream,
-        quarters(hat),
-        quarters(gain_row[None]),
-        quarters(router_row[None]),
-        scalars,
-        w_gate[0],
-        w_up[0],
-        w_down[0],
-    )
-    gathered = results[:6]
+        route_blocks, route_dest, saved, grad_out, gain, w_router, w_gate, w_up, w_down
+    )
     hid, gg, ug, nb, fresh, stats = results[6:]
-    grads = weight_grads(hid, gg, ug, gathered, w_gate.shape[1], model_dim)
-
-    def whole(rows):
-        return rows[:, :, :QUARTER].transpose(1, 0, 2).reshape(2, BLOCK, model_dim)
-
-    above = whole(nb)
-    above_ids = nb[0, :: BLOCK, QUARTER].astype(jnp.int32)
-    own = whole(fresh)
-    ids = jnp.arange(block_count, dtype=jnp.int32)[:, None, None]
-    outcome = grad_out.reshape(block_count, BLOCK, model_dim)
-    for rows, where in (
-        (above[0], above_ids[0]),
-        (above[1], above_ids[1]),
-        (own[0], keep_block),
-        (own[1], hand_block),
-    ):
-        outcome = jnp.where(ids == where, rows[None], outcome)
-    by_row = stats[:, :QUARTER].reshape(RING, 2, QUARTER)
-    stat_gain = by_row[:, 0].reshape(model_dim) / gain_row
-    stat_router = by_row[:, 1].reshape(model_dim) / gain_row
-    return (
-        outcome.reshape(tok_rows, model_dim)[None],
-        grads[0][None],
-        grads[1][None],
-        grads[2][None],
-        stat_gain[None],
-        stat_router[None],
-    )
+    return tuple(finish(hid, gg, ug, results[:6], grad_out, nb, fresh, stats, gain))
 
 
 def solution(mesh):

time: 149 us -> 116 us (0.78)
  local copies, waits for them, and re-layouts: 23.2 us -> 0 us
  other arithmetic: 8.29 us -> 0 us
  between operations: 5.47 us -> 0.64 us
  Pallas kernels: 111 us -> 114 us
    unnamed x36 -> x0, local copies, waits for them, and re-layouts: 9.96 us -> none
    broadcast_in_dim x18 -> x0, local copies, waits for them, and re-layouts: 6.93 us -> none  [the longest x16 6.24 us: on_device(): outcome = jnp.where(ids == where, rows[None], outcome)]
    pallas_call x2, Pallas kernels: 111 us -> 114 us  [the longest x1 106 us: communicate(): pl.pallas_call(step_kernel, out_shape=out_shape, in_specs=[smem] * 2 + [h...]
    slice x8 -> x0, local copies, waits for them, and re-layouts: 3.26 us -> none  [the longest x1 1.31 us: on_device(): handed = jnp.where(kept, targets[1] >= 0, targets[0] >= 0)]
    select_n x1 -> x0, other arithmetic: 3.19 us -> none  [on_device(): outcome = jnp.where(ids == where, rows[None], outcome)]
where the time goes in v2:
time: 116 us; the launch traced here: 115 us
  Pallas kernels  114 us (98%)
    pallas_call x1, Pallas kernels, communicate(): pl.pallas_call(step_kernel, out_shape=out_shape, in_specs=[smem] * 2 + [h...  106 us
    pallas_call x1, Pallas kernels, finish(): pl.pallas_call(finish_kernel, grid=(RING,), out_shape=[shape((1, tok_rows...  8.56 us

profile of v2, /device:TPU:0, one launch (start us, length us, event | category | flops | bytes accessed | tf_op | source)
XLA Modules:
  0.0 114.8 jit_solution(5824288417258325575)
XLA Ops:
  0.6 105.6 %routed_step.1 = (bf16[4,4,4,16,384]{4,3,2,1,0:T(8,128)(2,1)}, bf16[4,4,4,16,384]{4,3,2,1,0:T(8,128)(2,1)}, bf16[4,4,4,16,384]{4,3,2,1,0:T(8,128)(2,1)}, bf16[4,...) custom-call(s32[1,1,2]{2,1,0:T(1,128)} %blocks.1, ...), custom_call_target="tpu_custom_call" | custom-call | tf_op jit(solution)/shard_map/routed_step/pallas_call | solution.py:580
  106.3 8.6 %finish.1 = (bf16[1,128,4096]{2,1,0:T(8,128)(2,1)}, f32[1,224,4096]{2,1,0:T(8,128)}, f32[1,224,4096]{2,1,0:T(8,128)}, f32[1,224,4096]{2,1,0:T(8,128)}, f32[1,4096]{1,0:T(1,128)}, /*index=5*/f32[1,4096]{1,0:T(1,128)}) custom-call(bf16[256,224]{1,0:T(8,128)(2,1)} %get-tuple-element.18.hid, bf16[256,224]{1,0:T(8,128)(2,1)} %get-tuple-element.19.gg, ...), custom_call_target="tpu_custom_call" | custom-call | tf_op jit(solution)/shard_map/finish/pallas_call | solution.py:639

commit v3 on v2

--- a/solution.py
+++ b/solution.py
@@ -27,12 +27,6 @@
     )
 
 
-def contract_first(left_side, right_side):
-    return lax.dot_general(
-        left_side, right_side, (((0,), (0,)), ((), ())), preferred_element_type=F32
-    )
-
-
 def hi_lo(value):
     hi = value.astype(BF16).astype(F32)
     return hi, value - hi
@@ -41,12 +35,12 @@
 def step_kernel(
     blocks, targets, saved_hbm, grad_hbm, gain_hbm, router_hbm, wg_hbm, wu_hbm, wd_hbm,
     go0, go1, go2, so0, so1, so2, hid_o, gg_o, ug_o, nb_o, new_o, st_o,
-    saved, grad_out, gain, router_row, hat_ref, up_ref, sc, bn,
-    bs, hn, hs, g0, g1, g2, s0, s1, s2, r0, r1, r2,
+    saved, grad_out, gain, router_row, gain_q, router_q, bn, bu, hn, hu, up_tile, new_tile,
+    above, g0, g1, g2, s0, s1, s2, r0, r1, r2,
     rb00, rb01, rb02, a00, a01, a02, rb10, rb11, rb12, a10, a11, a12, rb20, rb21, rb22,
     u, nb, srb, acc, wg, wu, wd,
     hand_send, hand_recv, ag_send, ag_recv, rs_send, rs_recv, st_send, st_recv,
-    un_send, un_recv, nb_send, nb_recv, local_sem,
+    un_send, un_recv, ab_send, ab_recv, nb_send, nb_recv, local_sem, go_sem,
 ):
     pipe = lax.axis_index("pipe")
     me = lax.axis_index("ctx")
@@ -57,7 +51,8 @@
     at = (yy, xx, zz)
     quartets = RING * RING
     next_base = lax.rem(quartet + 1, quartets) * RING
-    prev_last = lax.rem(quartet + quartets - 1, quartets) * RING + RING - 1
+    prev_base = lax.rem(quartet + quartets - 1, quartets) * RING
+    prev_last = prev_base + RING - 1
 
     def ring_index(dim, off):
         return lax.rem(at[dim] + RING - off, RING)
@@ -70,7 +65,8 @@
     def same_pipe(ctx):
         return {"pipe": pipe, "ctx": ctx}
 
-    partner = {"pipe": 1 - pipe, "ctx": me}
+    def other_pipe(ctx):
+        return {"pipe": 1 - pipe, "ctx": ctx}
 
     def remote(src, dst, send, recv, device):
         return pltpu.make_async_remote_copy(
@@ -82,6 +78,11 @@
     rb0, a0 = (rb00, rb01, rb02), (a00, a01, a02)
     rb1, a1 = (rb10, rb11, rb12), (a10, a11, a12)
     rb2 = (rb20, rb21, rb22)
+
+    barrier = pltpu.get_barrier_semaphore()
+
+    def greet(device):
+        pl.semaphore_signal(barrier, inc=1, device_id=device, device_id_type=MESH)
 
     row_copies = [
         pltpu.make_async_copy(src, dst, local_sem.at[9 + i])
@@ -98,18 +99,13 @@
         pltpu.make_async_copy(src.at[0], dst, local_sem.at[i])
         for i, (src, dst) in enumerate(((wg_hbm, wg), (wu_hbm, wu), (wd_hbm, wd)))
     ]
-    for copy in row_copies + weight_copies:
+    for copy in row_copies:
         copy.start()
-
-    barrier = pltpu.get_barrier_semaphore()
-
-    def greet(device):
-        pl.semaphore_signal(barrier, inc=1, device_id=device, device_id_type=MESH)
-
     for dim in range(3):
         for off in OFFS:
             greet(peer(dim, off))
-    greet(partner)
+    for base in (prev_base, quartet * RING, next_base):
+        greet(other_pipe(base + yy))
     greet(same_pipe(prev_last))
 
     @pl.when(yy == RING - 1)
@@ -125,11 +121,10 @@
     mask = jnp.where(
         first_rows, jnp.where(kept, 1.0, 0.0).astype(F32), jnp.where(handed, 1.0, 0.0).astype(F32)
     )
-
     block_id = jnp.where(first_rows, keep_block, hand_block)
     row_in_block = lax.rem(lax.broadcasted_iota(jnp.int32, (2 * BLOCK, 1), 0), BLOCK)
     tokens = lax.broadcasted_iota(jnp.int32, (2 * BLOCK, saved.shape[0]), 1)
-    chosen = jnp.where(tokens == block_id * BLOCK + row_in_block, 1.0, 0.0).astype(BF16)
+    chosen = jnp.where(tokens == block_id * BLOCK + row_in_block, mask, 0.0).astype(BF16)
 
     def pick(array, cols):
         return jnp.dot(chosen, array[:, cols], preferred_element_type=F32)
@@ -141,29 +136,35 @@
         copy.wait()
     squares = jnp.zeros((2 * BLOCK, 1), F32)
     logits = jnp.zeros((2 * BLOCK, 1), F32)
+    picked = []
     for q in range(RING):
         rows = pick(saved, quarter(q))
-        hat_ref[q] = rows
+        picked.append(rows)
+        gain_q[q] = gain[:, quarter(q)]
+        router_q[q] = router_row[:, quarter(q)].astype(F32)
         squares += jnp.sum(rows * rows, axis=1, keepdims=True)
-        logits += jnp.sum(rows * router_row[:, quarter(q)].astype(F32), axis=1, keepdims=True)
+        logits += jnp.sum(rows * router_q[q], axis=1, keepdims=True)
     inverse = lax.rsqrt(squares / float(RING * QUARTER) + EPSILON)
     router = jax.nn.sigmoid(logits)
-    rest = (1.0 - router) * mask
-    carried_hi, carried_lo = hi_lo(rest / inverse)
     lane = lax.broadcasted_iota(jnp.int32, (2 * BLOCK, EXTRA), 1)
-    extra = jnp.where(lane == 0, carried_hi, jnp.where(lane == 1, carried_lo, 0.0)).astype(BF16)
+    extra = jnp.zeros((2 * BLOCK, EXTRA), F32)
+    for i, value in enumerate(
+        hi_lo((1.0 - router) / inverse)
+        + hi_lo(inverse)
+        + hi_lo(router)
+        + (block_id.astype(F32), me.astype(F32))
+    ):
+        extra = jnp.where(lane == i, value * mask, extra)
     for q in range(RING):
-        hat = hat_ref[q] * inverse
-        hat_ref[q] = hat
-        bn[q, :, :QUARTER] = (hat * gain[:, quarter(q)] * mask).astype(BF16)
-        bn[q, :, QUARTER:] = extra
-    for i, value in enumerate((router * mask, rest, inverse * mask, block_id.astype(F32))):
-        sc[i] = jnp.broadcast_to(value, (2 * BLOCK, EXTRA))
+        bn[q, :, :QUARTER] = (picked[q] * inverse * gain_q[q]).astype(BF16)
+        bn[q, :, QUARTER:] = extra.astype(BF16)
     row_copies[3].wait()
     for q in range(RING):
-        up_ref[q] = pick(grad_out, quarter(q))
-
-    pl.semaphore_wait(barrier, 11 + RING * lax.div(yy, RING - 1))
+        bu[q] = pick(grad_out, quarter(q)).astype(BF16)
+    for copy in weight_copies:
+        copy.start()
+
+    pl.semaphore_wait(barrier, 13 + RING * lax.div(yy, RING - 1))
 
     def hand_copies(src, dst, which):
         return [
@@ -191,25 +192,28 @@
 
         dst[yy + 1] = src[yy]
 
-    def hand_wait(src, dst, which):
+    def hand_recv_wait(src, dst, which):
         for copy in hand_copies(src, dst, which):
-            copy.wait()
+            copy.wait_recv()
         hand_over_copy(src, dst, which, 0).wait_recv()
+
+    def hand_send_wait(src, dst, which):
+        for copy in hand_copies(src, dst, which):
+            copy.wait_send()
 
         @pl.when(yy == RING - 1)
         def _():
             for j in range(RING):
                 hand_over_copy(src, dst, which, j).wait_send()
 
-    def make_tile(held, bufs, widths):
-        for k in range(3):
-            cols = slice(STARTS[k], STARTS[k] + widths[k])
-            b = [held[i, :, cols].astype(F32) for i in range(5)]
-            low = lax.broadcasted_iota(jnp.int32, b[0].shape, 0) < BLOCK
-            turned = [pltpu.roll(b[i], BLOCK, 0) for i in (0, 2, 4)]
-            top = b[1] + jnp.where(low, turned[0], turned[1])
-            bottom = b[3] + jnp.where(low, turned[1], turned[2])
-            bufs[k][yy, xx, zz] = jnp.concatenate([top, bottom], axis=0).astype(BF16)
+    def halves(held, cols):
+        b = [held[i, :, cols].astype(F32) for i in range(5)]
+        low = lax.broadcasted_iota(jnp.int32, b[0].shape, 0) < BLOCK
+        turned = [pltpu.roll(b[i], BLOCK, 0) for i in (0, 2, 4)]
+        return (
+            b[1] + jnp.where(low, turned[0], turned[1]),
+            b[3] + jnp.where(low, turned[1], turned[2]),
+        )
 
     def ag_copies(bufs, which, k, stage):
         dim = ORDERS[k][stage]
@@ -239,42 +243,59 @@
                 for copy in ag_copies(bufs, which, k, stage):
                     copy.wait_send()
 
+    def group(k):
+        return slice(STARTS[k], STARTS[k] + FEATS[k])
+
+    def tile_info():
+        info = g2[yy, xx, zz, :, FEATS[2] :].astype(F32)
+        return info, info[:, 4:5] + info[:, 5:6]
+
     def make_scaled():
-        for q in range(RING):
-            bs[q] = (sc[0][:, 0:1] * up_ref[q]).astype(BF16)
+        _, chance = tile_info()
+        for k in range(3):
+            rows = jnp.concatenate([up_tile[0, :, group(k)], up_tile[1, :, group(k)]], axis=0)
+            ss[k][yy, xx, zz] = (chance * rows).astype(BF16)
+            ag_start(ss, 1, k, 0)
+
+    def go_on(bufs, which, stage):
+        for k in range(3):
+            ag_recv_wait(bufs, which, k, stage - 1)
+            ag_start(bufs, which, k, stage)
+
+    hand_start(bn, hn, 0)
+    hand_start(bu, hu, 1)
+    hand_recv_wait(bn, hn, 0)
+    for k in range(3):
+        tile = halves(hn, slice(STARTS[k], STARTS[k] + WIDTHS[k]))
+        gs[k][yy, xx, zz] = jnp.concatenate(tile, axis=0).astype(BF16)
+
+        @pl.when(pipe == 1)
+        def _(k=k):
+            ag_start(gs, 0, k, 0)
+
+    hand_recv_wait(bu, hu, 1)
+    for k in range(3):
+        tile = halves(hu, group(k))
+        for h in range(2):
+            up_tile[h, :, group(k)] = tile[h]
 
     @pl.when(pipe == 1)
     def _():
         make_scaled()
-
-    hand_start(bn, hn, 0)
-
-    @pl.when(pipe == 1)
-    def _():
-        hand_start(bs, hs, 1)
-
-    hand_wait(bn, hn, 0)
-    make_tile(hn, gs, WIDTHS)
-    for k in range(3):
-        ag_start(gs, 0, k, 0)
-
-    @pl.when(pipe == 1)
-    def _():
-        hand_wait(bs, hs, 1)
-        make_tile(hs, ss, FEATS)
+        for stage in (1, 2):
+            go_on(gs, 0, stage)
+            go_on(ss, 1, stage)
+        pl.semaphore_signal(
+            go_sem, inc=1, device_id=other_pipe(me), device_id_type=MESH
+        )
+
+    @pl.when(pipe == 0)
+    def _():
+        pl.semaphore_wait(go_sem, 1)
         for k in range(3):
-            ag_start(ss, 1, k, 0)
-
-    for stage in (1, 2):
-        for k in range(3):
-            ag_recv_wait(gs, 0, k, stage - 1)
-            ag_start(gs, 0, k, stage)
-
-        @pl.when(pipe == 1)
-        def _(stage=stage):
-            for k in range(3):
-                ag_recv_wait(ss, 1, k, stage - 1)
-                ag_start(ss, 1, k, stage)
+            ag_start(gs, 0, k, 0)
+        for stage in (1, 2):
+            go_on(gs, 0, stage)
 
     for copy in weight_copies:
         copy.wait()
@@ -308,32 +329,59 @@
             acc[0] += gate_sum
             acc[1] += up_sum
 
-    def nb_copy():
-        return remote(new_o, nb, nb_send, nb_recv, partner)
+    def above_copies():
+        return [
+            remote(
+                new_tile, above.at[slot], ab_send.at[slot], ab_recv.at[slot],
+                other_pipe(base + yy),
+            )
+            for slot, base in ((2, prev_base), (1, quartet * RING), (0, next_base))
+        ]
 
     @pl.when(pipe == 0)
     def _():
-        nb_copy().wait_recv()
-        low = lax.broadcasted_iota(jnp.int32, (2 * BLOCK, 1), 0) < BLOCK
-        mine = sc[3][:, 0:1]
-        same = 1.0 - jnp.minimum(jnp.abs(nb[0, :, QUARTER : QUARTER + 1].astype(F32) - mine), 1.0)
-        other = pltpu.roll(nb[0, :, QUARTER:].astype(F32), BLOCK, 0)[:, 0:1]
-        cross = 1.0 - jnp.minimum(jnp.abs(other - mine), 1.0)
-        for q in range(RING):
-            rows = nb[q, :, :QUARTER].astype(F32)
-            turned = pltpu.roll(rows, BLOCK, 0)
-            kept_rows = (1.0 - same - cross) * up_ref[q]
-            up_ref[q] = same * rows + cross * turned + kept_rows
+        for copy in above_copies():
+            copy.wait_recv()
+        info, _ = tile_info()
+
+        def shifted(cols):
+            own = [above[1, h, :, cols].astype(F32) for h in range(2)]
+            ends = [above[0, 1, :, cols].astype(F32), above[2, 0, :, cols].astype(F32)]
+            turned = [pltpu.roll(v, BLOCK, 0) for v in (ends[0], own[0], own[1], ends[1])]
+            low = lax.broadcasted_iota(jnp.int32, own[0].shape, 0) < BLOCK
+            return [
+                (
+                    jnp.where(low, turned[h], turned[h + 1]),
+                    own[h],
+                    jnp.where(low, turned[h + 1], turned[h + 2]),
+                )
+                for h in range(2)
+            ]
+
+        ids = shifted(slice(QUARTER, QUARTER + EXTRA))
+        weights = []
+        for h in range(2):
+            mine = info[8 * h : 8 * h + 8, 6:8]
+            weights.append(
+                [
+                    1.0
+                    - jnp.minimum(
+                        jnp.abs(one[:, 6:7] - mine[:, 0:1]) + jnp.abs(one[:, 7:8] - mine[:, 1:2]),
+                        1.0,
+                    )
+                    for one in ids[h]
+                ]
+            )
+        for k in range(3):
+            for h, rows in enumerate(shifted(group(k))):
+                w = weights[h]
+                value = (1.0 - w[0] - w[1] - w[2]) * up_tile[h, :, group(k)]
+                for part, one in zip(w, rows):
+                    value += part * one
+                up_tile[h, :, group(k)] = value
         make_scaled()
-        hand_start(bs, hs, 1)
-        hand_wait(bs, hs, 1)
-        make_tile(hs, ss, FEATS)
-        for k in range(3):
-            ag_start(ss, 1, k, 0)
         for stage in (1, 2):
-            for k in range(3):
-                ag_recv_wait(ss, 1, k, stage - 1)
-                ag_start(ss, 1, k, stage)
+            go_on(ss, 1, stage)
 
     for k in range(3):
         ag_recv_wait(ss, 1, k, 2)
@@ -354,15 +402,19 @@
     activated = gate_pre * sigma
     slope = sigma * (1.0 + gate_pre * (1.0 - sigma))
     hidden = (activated * up_value).astype(BF16)
-    hid_o[...] = hidden
     row_part = jnp.sum(hidden_grad * hidden.astype(F32), axis=1, keepdims=True)
-    gg_o[...] = (hidden_grad * up_value * slope).astype(BF16)
-    ug_o[...] = (hidden_grad * activated).astype(BF16)
+    gg = (hidden_grad * up_value * slope).astype(BF16)
+    ug = (hidden_grad * activated).astype(BF16)
+    dot_part = jnp.sum(
+        gg.astype(F32) * gate_pre + ug.astype(F32) * up_value, axis=1, keepdims=True
+    )
     extra = g2[0, :, :, :, FEATS[2] :].reshape(quartets * ROWS, EXTRA).astype(F32)
-    weight = row_part * jnp.sum(extra, axis=1, keepdims=True)
-    row_hi, row_lo = hi_lo(row_part)
+    weight = row_part * (extra[:, 0:1] + extra[:, 1:2])
     lane = lax.broadcasted_iota(jnp.int32, (quartets * ROWS, EXTRA), 1)
-    row_lanes = jnp.where(lane == 0, row_hi, jnp.where(lane == 1, row_lo, 0.0)).astype(BF16)
+    row_lanes = jnp.zeros((quartets * ROWS, EXTRA), F32)
+    for i, value in enumerate(hi_lo(row_part) + hi_lo(dot_part)):
+        row_lanes = jnp.where(lane == i, value, row_lanes)
+    row_lanes = row_lanes.astype(BF16).reshape(RING, RING, ROWS, EXTRA)
 
     def rs_copies(k, stage):
         order = ORDERS[k]
@@ -399,8 +451,6 @@
         )
 
     srb[0, yy] = jnp.zeros((2 * RING, QUARTER + EXTRA), F32)
-    gg = gg_o[...]
-    ug = ug_o[...]
     for k in range(3):
         for q in range(RING):
             part = jnp.dot(gg, wg[:, columns(k, q)], preferred_element_type=F32) + jnp.dot(
@@ -409,11 +459,10 @@
             shape = (RING, RING, ROWS, FEATS[k])
             rs[k][q, :, :, :, : FEATS[k]] = part.astype(BF16).reshape(shape)
             if k == 2:
-                rs[k][q, :, :, :, FEATS[k] :] = row_lanes.reshape(RING, RING, ROWS, EXTRA)
+                rs[k][q, :, :, :, FEATS[k] :] = row_lanes
             rows = rows_of(gs, k, q).astype(F32)
-            cols = slice(STARTS[k], STARTS[k] + FEATS[k])
-            srb[0, yy, 2 * q : 2 * q + 1, cols] = jnp.sum(part * rows, axis=0, keepdims=True)
-            srb[0, yy, 2 * q + 1 : 2 * q + 2, cols] = jnp.sum(
+            srb[0, yy, 2 * q : 2 * q + 1, group(k)] = jnp.sum(part * rows, axis=0, keepdims=True)
+            srb[0, yy, 2 * q + 1 : 2 * q + 2, group(k)] = jnp.sum(
                 weight * rows, axis=0, keepdims=True
             )
         rs_start(k, 0)
@@ -434,6 +483,8 @@
 
     for copy in st_copies(0):
         copy.start()
+    for ref, value in ((hid_o, hidden), (gg_o, gg), (ug_o, ug)):
+        ref[...] = value.astype(F32).T.astype(BF16)
     for stage in (0, 1):
         for k in range(3):
             (a0, a1)[stage][k][...] = rs_sum(k, stage)
@@ -441,67 +492,75 @@
         srb[stage + 1, at[stage + 1]] = st_sum(stage)
         for copy in st_copies(stage + 1):
             copy.start()
+
+    sums = [rs_sum(k, 2) for k in range(3)]
+    info, chance = tile_info()
+    spare = sums[2][:, FEATS[2] :]
+    logit_grad = (spare[:, 0:1] + spare[:, 1:2]) * (1.0 - chance)
+    mean = (spare[:, 2:3] + spare[:, 3:4]) / float(RING * QUARTER)
+    scale = info[:, 2:3] + info[:, 3:4]
     for k in range(3):
-        u[yy, 0:ROWS, STARTS[k] : STARTS[k] + WIDTHS[k]] = rs_sum(k, 2)
+        gain_row = gain_q[yy, :, group(k)]
+        hat = gs[k][yy, xx, zz, :, : FEATS[k]].astype(F32) / gain_row
+        delta = scale * (sums[k][:, : FEATS[k]] * gain_row - hat * mean)
+        delta = delta + logit_grad * router_q[yy, :, group(k)]
+        for h in range(2):
+            half = delta[8 * h : 8 * h + 8]
+            new_tile[h, :, group(k)] = (up_tile[h, :, group(k)] + half).astype(BF16)
+    for h in range(2):
+        new_tile[h, :, QUARTER:] = info[8 * h : 8 * h + 8].astype(BF16)
+
+    @pl.when(pipe == 1)
+    def _():
+        for copy in above_copies():
+            copy.start()
 
     def back_copies():
         return [
             remote(
-                u.at[yy, pl.ds(0, ROWS)], u.at[yy, pl.ds(0, ROWS)],
-                un_send.at[off], un_recv.at[off], peer(0, off),
+                new_tile, u.at[yy, pl.ds(0, 2)], un_send.at[off], un_recv.at[off], peer(0, off)
             )
             for off in OFFS
         ]
 
     def back_over_copy(q):
         return remote(
-            u.at[yy, pl.ds(0, 8)], u.at[yy, pl.ds(ROWS, 8)],
-            un_send.at[0], un_recv.at[RING + q], same_pipe(prev_last),
-        )
-
-    def back_over_wait(q):
-        return remote(
-            u.at[q, pl.ds(0, 8)], u.at[q, pl.ds(ROWS, 8)],
-            un_send.at[0], un_recv.at[RING + q], same_pipe(prev_last),
+            new_tile, u.at[q, pl.ds(2, 2)], un_send.at[0], un_recv.at[RING + q],
+            same_pipe(prev_last),
         )
 
     for copy in back_copies():
         copy.start()
     back_over_copy(yy).start()
+    u[yy, 0:2] = new_tile[...]
+    st_o[...] = st_sum(2)
     for copy in back_copies():
         copy.wait_recv()
 
     @pl.when(yy == RING - 1)
     def _():
         for q in range(RING):
-            back_over_wait(q).wait_recv()
-
-    first = pl.multiple_of(lax.div(yy, 2) * 8, 8)
+            back_over_copy(q).wait_recv()
+
+    upper = lax.div(yy, 2)
     odd = lax.rem(yy, 2) == 1
 
     def owned(q, cols):
-        a = u[q, pl.ds(first, 8), cols]
-        b = u[q, pl.ds(first + 8, 8), cols]
+        a = u[q, upper, :, cols].astype(F32)
+        b = u[q, upper + 1, :, cols].astype(F32)
         low = lax.broadcasted_iota(jnp.int32, a.shape, 0) < BLOCK
         turned = jnp.where(low, pltpu.roll(a, BLOCK, 0), pltpu.roll(b, BLOCK, 0))
         return jnp.where(odd, turned, a)
 
-    feats = slice(0, QUARTER)
-    total = jnp.zeros((2 * BLOCK, 1), F32)
+    ids = owned(0, slice(QUARTER, QUARTER + EXTRA))
+    valid = jnp.abs(ids[:, 7:8] - me.astype(F32)) < 0.5
+    which = jnp.broadcast_to(jnp.where(valid, ids[:, 6:7], -1.0), (2 * BLOCK, EXTRA))
     for q in range(RING):
-        hat_grad = owned(q, feats) * gain[:, quarter(q)]
-        total = total + jnp.sum(hat_grad * hat_ref[q], axis=1, keepdims=True)
-    mean = total / float(RING * QUARTER)
-    row_sum = jnp.sum(owned(0, slice(QUARTER, QUARTER + EXTRA)), axis=1, keepdims=True)
-    logit_grad = row_sum * sc[1][:, 0:1]
-    scale = sc[2][:, 0:1]
-    for q in range(RING):
-        hat_grad = owned(q, feats) * gain[:, quarter(q)]
-        delta = scale * (hat_grad - hat_ref[q] * mean) + logit_grad * router_row[
-            :, quarter(q)
-        ].astype(F32)
-        new_o[q, :, :QUARTER] = (up_ref[q] + delta).astype(BF16)
-        new_o[q, :, QUARTER:] = sc[3].astype(BF16)
+        new_o[q, :, :QUARTER] = owned(q, slice(0, QUARTER)).astype(BF16)
+        new_o[q, :, QUARTER:] = which.astype(BF16)
+
+    def nb_copy():
+        return remote(new_o, nb, nb_send, nb_recv, other_pipe(me))
 
     @pl.when(pipe == 1)
     def _():
@@ -510,10 +569,11 @@
 
     @pl.when(pipe == 0)
     def _():
+        nb_copy().wait_recv()
         nb_o[...] = nb[...]
 
-    st_o[...] = st_sum(2)
-
+    hand_send_wait(bn, hn, 0)
+    hand_send_wait(bu, hu, 1)
     ag_send_wait(gs, 0)
     ag_send_wait(ss, 1)
     for k in range(3):
@@ -526,6 +586,8 @@
 
     @pl.when(pipe == 1)
     def _():
+        for copy in above_copies():
+            copy.wait_send()
         nb_copy().wait_send()
 
     for copy in gathered_out:
@@ -544,7 +606,7 @@
     out_shape = (
         [shape(cube + (w,), BF16) for w in WIDTHS]
         + [shape(cube + (w,), BF16) for w in FEATS]
-        + [shape((rows, ff), BF16)] * 3
+        + [shape((ff, rows), BF16)] * 3
         + [shape((RING, 8, width), BF16)] * 2
         + [shape((8, width), F32)]
     )
@@ -552,10 +614,11 @@
     scratch = (
         [pltpu.VMEM(grad_out.shape, BF16)] * 2
         + [pltpu.VMEM(gain.shape, F32), pltpu.VMEM(w_router.shape, BF16)]
-        + [pltpu.VMEM((RING, 8, QUARTER), F32)] * 2
-        + [pltpu.VMEM((4, 8, EXTRA), F32), pltpu.VMEM((RING, 8, width), BF16)]
-        + [pltpu.VMEM((RING, 8, QUARTER), BF16)]
+        + [pltpu.VMEM((RING, 1, QUARTER), F32)] * 2
+        + [pltpu.VMEM((RING, 8, width), BF16), pltpu.VMEM((RING, 8, QUARTER), BF16)]
         + [pltpu.VMEM((5, 8, width), BF16), pltpu.VMEM((5, 8, QUARTER), BF16)]
+        + [pltpu.VMEM((2, 8, QUARTER), F32), pltpu.VMEM((2, 8, width), BF16)]
+        + [pltpu.VMEM((3, 2, 8, width), BF16)]
         + [pltpu.VMEM(cube + (w,), BF16) for w in WIDTHS]
         + [pltpu.VMEM(cube + (w,), BF16) for w in FEATS]
         + [pltpu.VMEM(cube + (w,), BF16) for w in WIDTHS]
@@ -564,7 +627,7 @@
         + [pltpu.VMEM((3, RING, ROWS, w), F32) for w in WIDTHS]
         + [pltpu.VMEM((RING, ROWS, w), F32) for w in WIDTHS]
         + [pltpu.VMEM((3, ROWS, w), F32) for w in WIDTHS]
-        + [pltpu.VMEM((RING, ROWS + 8, width), F32)]
+        + [pltpu.VMEM((RING, 4, 8, width), BF16)]
         + [pltpu.VMEM((RING, 8, width), BF16)]
         + [pltpu.VMEM((3, RING, 8, width), F32)]
         + [pltpu.VMEM((3, rows, ff), F32)]
@@ -574,8 +637,9 @@
         + [dma((3, 3, 4)), dma((3, 3, 4))]
         + [dma((3, 4)), dma((3, 4))]
         + [dma((4,)), dma((8,))]
+        + [dma((3,)), dma((3,))]
         + [dma, dma]
-        + [dma((13,))]
+        + [dma((13,)), pltpu.SemaphoreType.REGULAR]
     )
     return pl.pallas_call(
         step_kernel,
@@ -594,14 +658,14 @@
     hid, gg, ug, g0, g1, g2, s0, s1, s2, grad_out, nb, fresh, stats, gain,
     out_inputs, out_gate, out_up, out_down, out_gain, out_router,
 ):
-    rows = hid.shape[0]
+    rows = hid.shape[1]
     for k, (g, s) in enumerate(zip((g0, g1, g2), (s0, s1, s2))):
         cols = slice(STARTS[k], STARTS[k] + FEATS[k])
         normed = g[0, :, :, :, : FEATS[k]].reshape(rows, FEATS[k])
         scaled = s[0].reshape(rows, FEATS[k])
-        out_gate[0, :, cols] = contract_first(gg[...], normed)
-        out_up[0, :, cols] = contract_first(ug[...], normed)
-        out_down[0, :, cols] = contract_first(hid[...], scaled)
+        out_gate[0, :, cols] = jnp.dot(gg[...], normed, preferred_element_type=F32)
+        out_up[0, :, cols] = jnp.dot(ug[...], normed, preferred_element_type=F32)
+        out_down[0, :, cols] = jnp.dot(hid[...], scaled, preferred_element_type=F32)
     patterns = []
     low = lax.broadcasted_iota(jnp.int32, (2 * BLOCK, QUARTER), 0) < BLOCK
     for ref in (nb, fresh):
@@ -624,7 +688,7 @@
 
 def finish(hid, gg, ug, gathered, grad_out, nb, fresh, stats, gain):
     tok_rows, model_dim = grad_out.shape
-    ff = hid.shape[1]
+    ff = hid.shape[0]
 
     def whole(array):
         return pl.BlockSpec(array.shape, lambda q: (0,) * array.ndim)

time: 116 us -> 106 us (0.914)
  Pallas kernels: 114 us -> 105 us
    pallas_call x1, Pallas kernels: 106 us -> 96.8 us  [communicate(): pl.pallas_call(step_kernel, out_shape=out_shape, in_specs=[smem] * 2 + [h...]
where the time goes in v3:
time: 106 us
  Pallas kernels  105 us (99%)
    pallas_call x1, Pallas kernels, communicate(): pl.pallas_call(step_kernel, out_shape=out_shape, in_specs=[smem] * 2 + [h...  96.8 us
    pallas_call x1, Pallas kernels, finish(): pl.pallas_call(finish_kernel, grid=(RING,), out_shape=[shape((1, tok_rows...  8.43 us

profile of v3, /device:TPU:0, one launch (start us, length us, event | category | flops | bytes accessed | tf_op | source)
XLA Modules:
  0.0 105.8 jit_solution(11553118638984718733)
XLA Ops:
  0.6 96.8 %routed_step.1 = (bf16[4,4,4,16,384]{4,3,2,1,0:T(8,128)(2,1)}, bf16[4,4,4,16,384]{4,3,2,1,0:T(8,128)(2,1)}, bf16[4,4,4,16,384]{4,3,2,1,0:T(8,128)(2,1)}, bf16[4,...) custom-call(s32[1,1,2]{2,1,0:T(1,128)} %blocks.1, ...), custom_call_target="tpu_custom_call" | custom-call | tf_op jit(solution)/shard_map/routed_step/pallas_call | solution.py:644
  97.4 8.4 %finish.1 = (bf16[1,128,4096]{2,1,0:T(8,128)(2,1)}, f32[1,224,4096]{2,1,0:T(8,128)}, f32[1,224,4096]{2,1,0:T(8,128)}, f32[1,224,4096]{2,1,0:T(8,128)}, f32[1,4096]{1,0:T(1,128)}, /*index=5*/f32[1,4096]{1,0:T(1,128)}) custom-call(bf16[224,256]{1,0:T(8,128)(2,1)} %get-tuple-element.18.hid, bf16[224,256]{1,0:T(8,128)(2,1)} %get-tuple-element.19.gg, ...), custom_call_target="tpu_custom_call" | custom-call | tf_op jit(solution)/shard_map/finish/pallas_call | solution.py:703

commit v4 on v3

--- a/solution.py
+++ b/solution.py
@@ -34,7 +34,7 @@
 
 def step_kernel(
     blocks, targets, saved_hbm, grad_hbm, gain_hbm, router_hbm, wg_hbm, wu_hbm, wd_hbm,
-    go0, go1, go2, so0, so1, so2, hid_o, gg_o, ug_o, nb_o, new_o, st_o,
+    gate_o, up_o, down_o, nb_o, new_o, st_o,
     saved, grad_out, gain, router_row, gain_q, router_q, bn, bu, hn, hu, up_tile, new_tile,
     above, g0, g1, g2, s0, s1, s2, r0, r1, r2,
     rb00, rb01, rb02, a00, a01, a02, rb10, rb11, rb12, a10, a11, a12, rb20, rb21, rb22,
@@ -158,12 +158,6 @@
     for q in range(RING):
         bn[q, :, :QUARTER] = (picked[q] * inverse * gain_q[q]).astype(BF16)
         bn[q, :, QUARTER:] = extra.astype(BF16)
-    row_copies[3].wait()
-    for q in range(RING):
-        bu[q] = pick(grad_out, quarter(q)).astype(BF16)
-    for copy in weight_copies:
-        copy.start()
-
     pl.semaphore_wait(barrier, 13 + RING * lax.div(yy, RING - 1))
 
     def hand_copies(src, dst, which):
@@ -263,7 +257,12 @@
             ag_start(bufs, which, k, stage)
 
     hand_start(bn, hn, 0)
+    row_copies[3].wait()
+    for q in range(RING):
+        bu[q] = pick(grad_out, quarter(q)).astype(BF16)
     hand_start(bu, hu, 1)
+    for copy in weight_copies:
+        copy.start()
     hand_recv_wait(bn, hn, 0)
     for k in range(3):
         tile = halves(hn, slice(STARTS[k], STARTS[k] + WIDTHS[k]))
@@ -306,14 +305,8 @@
     def columns(k, q):
         return slice(q * QUARTER + STARTS[k], q * QUARTER + STARTS[k] + FEATS[k])
 
-    gathered_out = [
-        pltpu.make_async_copy(src, dst, local_sem.at[3 + i])
-        for i, (src, dst) in enumerate(zip(gs + ss, (go0, go1, go2, so0, so1, so2)))
-    ]
-
     for k in range(3):
         ag_recv_wait(gs, 0, k, 2)
-        gathered_out[k].start()
         gate_sum = None
         up_sum = None
         for q in range(RING):
@@ -385,7 +378,6 @@
 
     for k in range(3):
         ag_recv_wait(ss, 1, k, 2)
-        gathered_out[3 + k].start()
         grad_sum = None
         for q in range(RING):
             part = contract_last(rows_of(ss, k, q), wd[:, columns(k, q)])
@@ -483,11 +475,18 @@
 
     for copy in st_copies(0):
         copy.start()
-    for ref, value in ((hid_o, hidden), (gg_o, gg), (ug_o, ug)):
-        ref[...] = value.astype(F32).T.astype(BF16)
+    turned = [value.astype(F32).T.astype(BF16) for value in (gg, ug, hidden)]
+    for q in range(RING):
+        for k in range(3):
+            normed = rows_of(gs, k, q)
+            gate_o[:, columns(k, q)] = jnp.dot(turned[0], normed, preferred_element_type=F32)
+            up_o[:, columns(k, q)] = jnp.dot(turned[1], normed, preferred_element_type=F32)
+            down_o[:, columns(k, q)] = jnp.dot(
+                turned[2], rows_of(ss, k, q), preferred_element_type=F32
+            )
     for stage in (0, 1):
         for k in range(3):
-            (a0, a1)[stage][k][...] = rs_sum(k, stage)
+            (a0, a1)[stage][k][...] = rs_sum(k, stage).astype(BF16)
             rs_start(k, stage + 1)
         srb[stage + 1, at[stage + 1]] = st_sum(stage)
         for copy in st_copies(stage + 1):
@@ -590,9 +589,6 @@
             copy.wait_send()
         nb_copy().wait_send()
 
-    for copy in gathered_out:
-        copy.wait()
-
 
 def communicate(route_blocks, route_dest, saved, grad_out, gain, w_router, wg, wu, wd):
     ff = wg.shape[1]
@@ -602,13 +598,10 @@
     smem = pl.BlockSpec(memory_space=pltpu.SMEM)
     hbm = pl.BlockSpec(memory_space=pl.ANY)
     cube = (RING, RING, RING, ROWS)
-    shape = jax.ShapeDtypeStruct
     out_shape = (
-        [shape(cube + (w,), BF16) for w in WIDTHS]
-        + [shape(cube + (w,), BF16) for w in FEATS]
-        + [shape((ff, rows), BF16)] * 3
-        + [shape((RING, 8, width), BF16)] * 2
-        + [shape((8, width), F32)]
+        [pltpu.VMEM((ff, grad_out.shape[1]), F32)] * 3
+        + [pltpu.VMEM((RING, 8, width), BF16)] * 2
+        + [pltpu.VMEM((8, width), F32)]
     )
     dma = pltpu.SemaphoreType.DMA
     scratch = (
@@ -623,10 +616,10 @@
         + [pltpu.VMEM(cube + (w,), BF16) for w in FEATS]
         + [pltpu.VMEM(cube + (w,), BF16) for w in WIDTHS]
         + [pltpu.VMEM((3, RING, RING, ROWS, w), BF16) for w in WIDTHS]
-        + [pltpu.VMEM((RING, RING, ROWS, w), F32) for w in WIDTHS]
-        + [pltpu.VMEM((3, RING, ROWS, w), F32) for w in WIDTHS]
-        + [pltpu.VMEM((RING, ROWS, w), F32) for w in WIDTHS]
-        + [pltpu.VMEM((3, ROWS, w), F32) for w in WIDTHS]
+        + [pltpu.VMEM((RING, RING, ROWS, w), BF16) for w in WIDTHS]
+        + [pltpu.VMEM((3, RING, ROWS, w), BF16) for w in WIDTHS]
+        + [pltpu.VMEM((RING, ROWS, w), BF16) for w in WIDTHS]
+        + [pltpu.VMEM((3, ROWS, w), BF16) for w in WIDTHS]
         + [pltpu.VMEM((RING, 4, 8, width), BF16)]
         + [pltpu.VMEM((RING, 8, width), BF16)]
         + [pltpu.VMEM((3, RING, 8, width), F32)]
@@ -645,85 +638,81 @@
         step_kernel,
         out_shape=out_shape,
         in_specs=[smem] * 2 + [hbm] * 7,
-        out_specs=[hbm] * 6 + [vmem] * 6,
+        out_specs=[vmem] * 6,
         scratch_shapes=scratch,
         compiler_params=pltpu.CompilerParams(
-            collective_id=0, has_side_effects=True, vmem_limit_bytes=58 * 1024 * 1024
+            collective_id=0, has_side_effects=True, vmem_limit_bytes=50 * 1024 * 1024
         ),
         name="routed_step",
     )(route_blocks, route_dest, saved, grad_out, gain, w_router, wg, wu, wd)
 
 
 def finish_kernel(
-    hid, gg, ug, g0, g1, g2, s0, s1, s2, grad_out, nb, fresh, stats, gain,
+    gate, up, down, grad_hbm, nb, fresh, stats, gain,
     out_inputs, out_gate, out_up, out_down, out_gain, out_router,
+    grad_out, outcome, sem,
 ):
-    rows = hid.shape[1]
-    for k, (g, s) in enumerate(zip((g0, g1, g2), (s0, s1, s2))):
-        cols = slice(STARTS[k], STARTS[k] + FEATS[k])
-        normed = g[0, :, :, :, : FEATS[k]].reshape(rows, FEATS[k])
-        scaled = s[0].reshape(rows, FEATS[k])
-        out_gate[0, :, cols] = jnp.dot(gg[...], normed, preferred_element_type=F32)
-        out_up[0, :, cols] = jnp.dot(ug[...], normed, preferred_element_type=F32)
-        out_down[0, :, cols] = jnp.dot(hid[...], scaled, preferred_element_type=F32)
-    patterns = []
+    load = pltpu.make_async_copy(grad_hbm, grad_out, sem.at[0])
+    load.start()
+    copies = [
+        pltpu.make_async_copy(src, dst.at[0], sem.at[1 + i])
+        for i, (src, dst) in enumerate(((gate, out_gate), (up, out_up), (down, out_down)))
+    ]
+    for copy in copies:
+        copy.start()
+    for q in range(RING):
+        cols = slice(q * QUARTER, (q + 1) * QUARTER)
+        out_gain[:, cols] = stats[2 * q : 2 * q + 1, :QUARTER] / gain[:, cols]
+        out_router[:, cols] = stats[2 * q + 1 : 2 * q + 2, :QUARTER] / gain[:, cols]
     low = lax.broadcasted_iota(jnp.int32, (2 * BLOCK, QUARTER), 0) < BLOCK
-    for ref in (nb, fresh):
-        new_rows = ref[0, :, :QUARTER].astype(F32)
-        turned = pltpu.roll(new_rows, BLOCK, 0)
-        which = ref[0, :, QUARTER:].astype(F32)
-        patterns.append((which[0:1, 0:1], jnp.where(low, new_rows, turned)))
-        patterns.append((which[BLOCK : BLOCK + 1, 0:1], jnp.where(low, turned, new_rows)))
     half = jnp.where(lax.broadcasted_iota(jnp.int32, (2 * BLOCK, 1), 0) < BLOCK, 0.0, 1.0)
-    for i in range(grad_out.shape[0] // 8):
-        block = half + float(2 * i)
-        value = grad_out[8 * i : 8 * i + 8, :].astype(F32)
-        for which, pattern in patterns:
-            value = jnp.where(block == which, pattern, value)
-        out_inputs[0, 8 * i : 8 * i + 8, :] = value.astype(BF16)
-    q = pl.program_id(0)
-    out_gain[...] = stats[pl.ds(2 * q, 1), :QUARTER] / gain[...]
-    out_router[...] = stats[pl.ds(2 * q + 1, 1), :QUARTER] / gain[...]
-
-
-def finish(hid, gg, ug, gathered, grad_out, nb, fresh, stats, gain):
+    load.wait()
+    for q in range(RING):
+        cols = slice(q * QUARTER, (q + 1) * QUARTER)
+        patterns = []
+        for ref in (nb, fresh):
+            new_rows = ref[q, :, :QUARTER].astype(F32)
+            turned = pltpu.roll(new_rows, BLOCK, 0)
+            which = ref[q, :, QUARTER:].astype(F32)
+            patterns.append((which[0:1, 0:1], jnp.where(low, new_rows, turned)))
+            patterns.append((which[BLOCK : BLOCK + 1, 0:1], jnp.where(low, turned, new_rows)))
+        for i in range(grad_out.shape[0] // 8):
+            block = half + float(2 * i)
+            value = grad_out[8 * i : 8 * i + 8, cols].astype(F32)
+            for which, pattern in patterns:
+                value = jnp.where(block == which, pattern, value)
+            outcome[8 * i : 8 * i + 8, cols] = value.astype(BF16)
+    store = pltpu.make_async_copy(outcome, out_inputs.at[0], sem.at[4])
+    store.start()
+    for copy in copies + [store]:
+        copy.wait()
+
+
+def finish(gate, up, down, grad_out, nb, fresh, stats, gain):
     tok_rows, model_dim = grad_out.shape
-    ff = hid.shape[0]
-
-    def whole(array):
-        return pl.BlockSpec(array.shape, lambda q: (0,) * array.ndim)
-
-    def part(width):
-        return pl.BlockSpec((1, RING, RING, ROWS, width), lambda q: (q, 0, 0, 0, 0))
-
-    new_rows = pl.BlockSpec((1,) + nb.shape[1:], lambda q: (q, 0, 0))
-    vector = pl.BlockSpec((1, QUARTER), lambda q: (0, q))
-    grads = pl.BlockSpec((1, ff, QUARTER), lambda q: (0, 0, q))
+    ff = gate.shape[0]
     shape = jax.ShapeDtypeStruct
+    vmem = pl.BlockSpec(memory_space=pltpu.VMEM)
+    hbm = pl.BlockSpec(memory_space=pl.ANY)
     return pl.pallas_call(
         finish_kernel,
-        grid=(RING,),
         out_shape=[shape((1, tok_rows, model_dim), BF16)]
         + [shape((1, ff, model_dim), F32)] * 3
         + [shape((1, model_dim), F32)] * 2,
-        in_specs=[whole(hid)] * 3
-        + [part(w) for w in WIDTHS + FEATS]
-        + [pl.BlockSpec((tok_rows, QUARTER), lambda q: (0, q)), new_rows, new_rows]
-        + [whole(stats), vector],
-        out_specs=[pl.BlockSpec((1, tok_rows, QUARTER), lambda q: (0, 0, q))]
-        + [grads] * 3
-        + [vector] * 2,
-        compiler_params=pltpu.CompilerParams(vmem_limit_bytes=60 * 1024 * 1024),
+        in_specs=[vmem] * 3 + [hbm] + [vmem] * 4,
+        out_specs=[hbm] * 4 + [vmem] * 2,
+        scratch_shapes=[pltpu.VMEM(grad_out.shape, BF16)] * 2
+        + [pltpu.SemaphoreType.DMA((5,))],
+        compiler_params=pltpu.CompilerParams(vmem_limit_bytes=8 * 1024 * 1024),
         name="finish",
-    )(hid, gg, ug, *gathered, grad_out, nb, fresh, stats, gain)
+    )(gate, up, down, grad_out, nb, fresh, stats, gain)
 
 
 def on_device(saved, grad_out, route_blocks, route_dest, gain, w_router, w_gate, w_up, w_down):
-    results = communicate(
+    gate, up, down, nb, fresh, stats = communicate(
         route_blocks, route_dest, saved, grad_out, gain, w_router, w_gate, w_up, w_down
     )
-    hid, gg, ug, nb, fresh, stats = results[6:]
-    return tuple(finish(hid, gg, ug, results[:6], grad_out, nb, fresh, stats, gain))
+    return tuple(finish(gate, up, down, grad_out, nb, fresh, stats, gain))
 
 
 def solution(mesh):

time: 106 us -> 100 us (0.943)
  Pallas kernels: 105 us -> 98.7 us
    pallas_call x1, Pallas kernels: 96.8 us -> 93.5 us  [communicate(): pl.pallas_call(step_kernel, out_shape=out_shape, in_specs=[smem] * 2 + [h...]
    pallas_call x1, Pallas kernels: 8.43 us -> 5.22 us  [finish(): pl.pallas_call(finish_kernel, out_shape=[shape((1, tok_rows, model_dim),...]
where the time goes in v4:
time: 100 us; the launch traced here: 99.4 us
  Pallas kernels  98.7 us (99%)
    pallas_call x1, Pallas kernels, communicate(): pl.pallas_call(step_kernel, out_shape=out_shape, in_specs=[smem] * 2 + [h...  93.5 us
    pallas_call x1, Pallas kernels, finish(): pl.pallas_call(finish_kernel, out_shape=[shape((1, tok_rows, model_dim),...  5.22 us

profile of v4, /device:TPU:0, one launch (start us, length us, event | category | flops | bytes accessed | tf_op | source)
XLA Modules:
  0.0 99.4 jit_solution(4839846691357600806)
XLA Ops:
  0.6 0.0 copy-start.1
  0.6 0.0 copy-start
  0.7 93.5 %routed_step.1 = (f32[224,4096]{1,0:T(8,128)S(1)}, f32[224,4096]{1,0:T(8,128)S(1)}, f32[224,4096]{1,0:T(8,128)S(1)}, bf16[4,8,1152]{2,1,0:T(8,128)(2,1)S(1)}, bf...) custom-call(s32[1,1,2]{2,1,0:T(1,128)} %blocks.1, s32[1,1,2]{2,1,0:T(1,128)} %targets.1, ...), custom_call_target="tpu_custom_call" | custom-call | tf_op jit(solution)/shard_map/routed_step/pallas_call | solution.py:637
  94.1 0.0 copy-done.1
  94.1 0.0 copy-done
  94.1 5.2 %finish.1 = (bf16[1,128,4096]{2,1,0:T(8,128)(2,1)}, f32[1,224,4096]{2,1,0:T(8,128)}, f32[1,224,4096]{2,1,0:T(8,128)}, f32[1,224,4096]{2,1,0:T(8,128)}, f32[1,4096]{1,0:T(1,128)}, /*index=5*/f32[1,4096]{1,0:T(1,128)}) custom-call(f32[224,4096]{1,0:T(8,128)S(1)} %get-tuple-element.12.gate, f32[224,4096]{1,0:T(8,128)S(1)} %get-tuple-element.13.up, ...), custom_call_target="tpu_custom_call" | custom-call | tf_op jit(solution)/shard_map/finish/pallas_call | solution.py:697
Async XLA Ops:
  0.6 93.5 %copy-start.1 = (f32[1,4096]{1,0:T(1,128)S(1)}, f32[1,4096]{1,0:T(1,128)}, u32[]{:S(2)}) copy-start(f32[1,4096]{1,0:T(1,128)} %gain.1) | copy-start | bytes 49156
  0.6 93.5 %copy-start = (bf16[128,4096]{1,0:T(8,128)(2,1)S(1)}, bf16[128,4096]{1,0:T(8,128)(2,1)}, u32[]{:S(2)}) copy-start(bf16[128,4096]{1,0:T(8,128)(2,1)} %grad_hbm.3) | copy-start | bytes 3145732

commit v5 on v4

--- a/solution.py
+++ b/solution.py
@@ -15,7 +15,9 @@
 FEATS = (384, 384, 256)
 STARTS = (0, 384, 768)
 ROWS = 16
-ORDERS = ((0, 1, 2), (1, 2, 0), (2, 0, 1))
+ALONG = (0, 1, 2)
+PLANES = ((1, 2), (0, 2), (0, 1))
+STEPS = tuple((i, j) for i in range(RING) for j in range(RING) if (i, j) != (0, 0))
 F32 = jnp.float32
 BF16 = jnp.bfloat16
 MESH = pl.DeviceIdType.MESH
@@ -37,7 +39,7 @@
     gate_o, up_o, down_o, nb_o, new_o, st_o,
     saved, grad_out, gain, router_row, gain_q, router_q, bn, bu, hn, hu, up_tile, new_tile,
     above, g0, g1, g2, s0, s1, s2, r0, r1, r2,
-    rb00, rb01, rb02, a00, a01, a02, rb10, rb11, rb12, a10, a11, a12, rb20, rb21, rb22,
+    rb00, rb01, rb02, a00, a01, a02, rb10, rb11, rb12,
     u, nb, srb, acc, wg, wu, wd,
     hand_send, hand_recv, ag_send, ag_recv, rs_send, rs_recv, st_send, st_recv,
     un_send, un_recv, ab_send, ab_recv, nb_send, nb_recv, local_sem, go_sem,
@@ -62,6 +64,12 @@
         pos[dim] = ring_index(dim, off)
         return {"pipe": pipe, "ctx": pos[1] * 16 + pos[2] * 4 + pos[0]}
 
+    def plane_peer(k, step):
+        pos = list(at)
+        for dim, off in zip(PLANES[k], step):
+            pos[dim] = ring_index(dim, off)
+        return {"pipe": pipe, "ctx": pos[1] * 16 + pos[2] * 4 + pos[0]}
+
     def same_pipe(ctx):
         return {"pipe": pipe, "ctx": ctx}
 
@@ -75,9 +83,9 @@
         )
 
     gs, ss, rs = (g0, g1, g2), (s0, s1, s2), (r0, r1, r2)
-    rb0, a0 = (rb00, rb01, rb02), (a00, a01, a02)
-    rb1, a1 = (rb10, rb11, rb12), (a10, a11, a12)
-    rb2 = (rb20, rb21, rb22)
+    rb0, rb1, a0 = (rb00, rb01, rb02), (rb10, rb11, rb12), (a00, a01, a02)
+    sb0 = (rb00, rb01, rb02.at[:, :, :, :, : FEATS[2]])
+    sb1 = (rb10, rb11, rb12.at[:, :, : FEATS[2]])
 
     barrier = pltpu.get_barrier_semaphore()
 
@@ -104,6 +112,9 @@
     for dim in range(3):
         for off in OFFS:
             greet(peer(dim, off))
+        for step in STEPS:
+            if step[0] and step[1]:
+                greet(plane_peer(dim, step))
     for base in (prev_base, quartet * RING, next_base):
         greet(other_pipe(base + yy))
     greet(same_pipe(prev_last))
@@ -158,7 +169,7 @@
     for q in range(RING):
         bn[q, :, :QUARTER] = (picked[q] * inverse * gain_q[q]).astype(BF16)
         bn[q, :, QUARTER:] = extra.astype(BF16)
-    pl.semaphore_wait(barrier, 13 + RING * lax.div(yy, RING - 1))
+    pl.semaphore_wait(barrier, 40 + RING * lax.div(yy, RING - 1))
 
     def hand_copies(src, dst, which):
         return [
@@ -210,15 +221,21 @@
         )
 
     def ag_copies(bufs, which, k, stage):
-        dim = ORDERS[k][stage]
-        index = tuple(
-            slice(None) if d in ORDERS[k][:stage] else at[d] for d in range(3)
-        )
+        if stage == 0:
+            tile = bufs[k].at[yy, xx, zz]
+            return [
+                remote(
+                    tile, tile, ag_send.at[which, k, 0], ag_recv.at[which, k, 0],
+                    plane_peer(k, step),
+                )
+                for step in STEPS
+            ]
+        index = tuple(at[d] if d == ALONG[k] else slice(None) for d in range(3))
+        tiles = bufs[k].at[index]
         return [
             remote(
-                bufs[k].at[index], bufs[k].at[index],
-                ag_send.at[which, k, stage, off], ag_recv.at[which, k, stage, off],
-                peer(dim, off),
+                tiles, tiles, ag_send.at[which, k, 1], ag_recv.at[which, k, 1],
+                peer(ALONG[k], off),
             )
             for off in OFFS
         ]
@@ -227,15 +244,23 @@
         for copy in ag_copies(bufs, which, k, stage):
             copy.start()
 
+    def ag_all(bufs, which, k, stage):
+        if stage == 0:
+            ref = (rb1, sb1)[which][k]
+        else:
+            ref = (rb0, sb0)[which][k]
+        return remote(
+            ref, ref, ag_send.at[which, k, stage], ag_recv.at[which, k, stage],
+            peer(ALONG[k], 1),
+        )
+
     def ag_recv_wait(bufs, which, k, stage):
-        for copy in ag_copies(bufs, which, k, stage):
-            copy.wait_recv()
+        ag_all(bufs, which, k, stage).wait_recv()
 
     def ag_send_wait(bufs, which):
         for k in range(3):
-            for stage in range(3):
-                for copy in ag_copies(bufs, which, k, stage):
-                    copy.wait_send()
+            for stage in range(2):
+                ag_all(bufs, which, k, stage).wait_send()
 
     def group(k):
         return slice(STARTS[k], STARTS[k] + FEATS[k])
@@ -251,10 +276,10 @@
             ss[k][yy, xx, zz] = (chance * rows).astype(BF16)
             ag_start(ss, 1, k, 0)
 
-    def go_on(bufs, which, stage):
+    def go_on(bufs, which):
         for k in range(3):
-            ag_recv_wait(bufs, which, k, stage - 1)
-            ag_start(bufs, which, k, stage)
+            ag_recv_wait(bufs, which, k, 0)
+            ag_start(bufs, which, k, 1)
 
     hand_start(bn, hn, 0)
     row_copies[3].wait()
@@ -281,9 +306,8 @@
     @pl.when(pipe == 1)
     def _():
         make_scaled()
-        for stage in (1, 2):
-            go_on(gs, 0, stage)
-            go_on(ss, 1, stage)
+        go_on(gs, 0)
+        go_on(ss, 1)
         pl.semaphore_signal(
             go_sem, inc=1, device_id=other_pipe(me), device_id_type=MESH
         )
@@ -293,8 +317,7 @@
         pl.semaphore_wait(go_sem, 1)
         for k in range(3):
             ag_start(gs, 0, k, 0)
-        for stage in (1, 2):
-            go_on(gs, 0, stage)
+        go_on(gs, 0)
 
     for copy in weight_copies:
         copy.wait()
@@ -306,7 +329,7 @@
         return slice(q * QUARTER + STARTS[k], q * QUARTER + STARTS[k] + FEATS[k])
 
     for k in range(3):
-        ag_recv_wait(gs, 0, k, 2)
+        ag_recv_wait(gs, 0, k, 1)
         gate_sum = None
         up_sum = None
         for q in range(RING):
@@ -322,6 +345,12 @@
             acc[0] += gate_sum
             acc[1] += up_sum
 
+    gate_pre = acc[0]
+    sigma = jax.nn.sigmoid(gate_pre)
+    activated = gate_pre * sigma
+    acc[3] = activated
+    acc[4] = acc[1] * sigma * (1.0 + gate_pre * (1.0 - sigma))
+
     def above_copies():
         return [
             remote(
@@ -373,11 +402,10 @@
                     value += part * one
                 up_tile[h, :, group(k)] = value
         make_scaled()
-        for stage in (1, 2):
-            go_on(ss, 1, stage)
+        go_on(ss, 1)
 
     for k in range(3):
-        ag_recv_wait(ss, 1, k, 2)
+        ag_recv_wait(ss, 1, k, 1)
         grad_sum = None
         for q in range(RING):
             part = contract_last(rows_of(ss, k, q), wd[:, columns(k, q)])
@@ -390,18 +418,15 @@
     gate_pre = acc[0]
     up_value = acc[1]
     hidden_grad = acc[2]
-    sigma = jax.nn.sigmoid(gate_pre)
-    activated = gate_pre * sigma
-    slope = sigma * (1.0 + gate_pre * (1.0 - sigma))
+    activated = acc[3]
     hidden = (activated * up_value).astype(BF16)
     row_part = jnp.sum(hidden_grad * hidden.astype(F32), axis=1, keepdims=True)
-    gg = (hidden_grad * up_value * slope).astype(BF16)
+    gg = (hidden_grad * acc[4]).astype(BF16)
     ug = (hidden_grad * activated).astype(BF16)
     dot_part = jnp.sum(
         gg.astype(F32) * gate_pre + ug.astype(F32) * up_value, axis=1, keepdims=True
     )
     extra = g2[0, :, :, :, FEATS[2] :].reshape(quartets * ROWS, EXTRA).astype(F32)
-    weight = row_part * (extra[:, 0:1] + extra[:, 1:2])
     lane = lax.broadcasted_iota(jnp.int32, (quartets * ROWS, EXTRA), 1)
     row_lanes = jnp.zeros((quartets * ROWS, EXTRA), F32)
     for i, value in enumerate(hi_lo(row_part) + hi_lo(dot_part)):
@@ -409,38 +434,49 @@
     row_lanes = row_lanes.astype(BF16).reshape(RING, RING, ROWS, EXTRA)
 
     def rs_copies(k, stage):
-        order = ORDERS[k]
-        dim = order[stage]
-        src = (rs, a0, a1)[stage][k]
-        dst = (rb0, rb1, rb2)[stage][k]
-        left = [d for d in range(3) if d not in order[:stage]]
-        copies = []
-        for off in OFFS:
-            index = tuple(ring_index(d, off) if d == dim else slice(None) for d in left)
-            copies.append(
-                remote(
-                    src.at[index], dst.at[off - 1],
-                    rs_send.at[k, stage, off], rs_recv.at[k, stage, off], peer(dim, off),
+        if stage == 0:
+            copies = []
+            for off in OFFS:
+                index = tuple(
+                    ring_index(d, off) if d == ALONG[k] else slice(None) for d in range(3)
                 )
-            )
-        return copies
+                copies.append(
+                    remote(
+                        rs[k].at[index], rb0[k].at[off - 1], rs_send.at[k, 0], rs_recv.at[k, 0],
+                        peer(ALONG[k], off),
+                    )
+                )
+            return copies
+        return [
+            remote(
+                a0[k].at[tuple(ring_index(d, off) for d, off in zip(PLANES[k], step))],
+                rb1[k].at[i], rs_send.at[k, 1], rs_recv.at[k, 1], plane_peer(k, step),
+            )
+            for i, step in enumerate(STEPS)
+        ]
 
     def rs_start(k, stage):
         for copy in rs_copies(k, stage):
             copy.start()
 
+    def rs_all(k, stage):
+        ref = (rb0, rb1)[stage][k]
+        return remote(
+            ref, ref, rs_send.at[k, stage], rs_recv.at[k, stage], peer(ALONG[k], 1)
+        )
+
     def rs_sum(k, stage):
-        for copy in rs_copies(k, stage):
-            copy.wait_recv()
-        order = ORDERS[k]
-        dim = order[stage]
-        src = (rs, a0, a1)[stage][k]
-        got = (rb0, rb1, rb2)[stage][k]
-        left = [d for d in range(3) if d not in order[:stage]]
-        index = tuple(at[d] if d == dim else slice(None) for d in left)
-        return (src[index].astype(F32) + got[0].astype(F32)) + (
-            got[1].astype(F32) + got[2].astype(F32)
-        )
+        rs_all(k, stage).wait_recv()
+        if stage == 0:
+            index = tuple(at[d] if d == ALONG[k] else slice(None) for d in range(3))
+            parts = [rs[k][index]] + [rb0[k][i] for i in range(3)]
+        else:
+            own = a0[k][tuple(at[d] for d in PLANES[k])]
+            parts = [own] + [rb1[k][i] for i in range(len(STEPS))]
+        parts = [part.astype(F32) for part in parts]
+        while len(parts) > 1:
+            parts = [parts[i] + parts[i + 1] for i in range(0, len(parts), 2)]
+        return parts[0]
 
     srb[0, yy] = jnp.zeros((2 * RING, QUARTER + EXTRA), F32)
     for k in range(3):
@@ -452,11 +488,6 @@
             rs[k][q, :, :, :, : FEATS[k]] = part.astype(BF16).reshape(shape)
             if k == 2:
                 rs[k][q, :, :, :, FEATS[k] :] = row_lanes
-            rows = rows_of(gs, k, q).astype(F32)
-            srb[0, yy, 2 * q : 2 * q + 1, group(k)] = jnp.sum(part * rows, axis=0, keepdims=True)
-            srb[0, yy, 2 * q + 1 : 2 * q + 2, group(k)] = jnp.sum(
-                weight * rows, axis=0, keepdims=True
-            )
         rs_start(k, 0)
 
     def st_copies(stage):
@@ -473,9 +504,11 @@
             copy.wait()
         return (srb[stage, 0] + srb[stage, 1]) + (srb[stage, 2] + srb[stage, 3])
 
-    for copy in st_copies(0):
-        copy.start()
     turned = [value.astype(F32).T.astype(BF16) for value in (gg, ug, hidden)]
+    weight_hi, weight_lo = hi_lo(row_part * (extra[:, 0:1] + extra[:, 1:2]))
+    lane = lax.broadcasted_iota(jnp.int32, (quartets * ROWS, EXTRA), 1)
+    weights = jnp.where(lane == 0, weight_hi, jnp.where(lane == 1, weight_lo, 0.0))
+    weights = weights.T[0:16].astype(BF16)
     for q in range(RING):
         for k in range(3):
             normed = rows_of(gs, k, q)
@@ -484,15 +517,31 @@
             down_o[:, columns(k, q)] = jnp.dot(
                 turned[2], rows_of(ss, k, q), preferred_element_type=F32
             )
-    for stage in (0, 1):
-        for k in range(3):
-            (a0, a1)[stage][k][...] = rs_sum(k, stage).astype(BF16)
-            rs_start(k, stage + 1)
-        srb[stage + 1, at[stage + 1]] = st_sum(stage)
-        for copy in st_copies(stage + 1):
-            copy.start()
-
-    sums = [rs_sum(k, 2) for k in range(3)]
+            srb[0, yy, 2 * q : 2 * q + 1, group(k)] = jnp.sum(
+                gate_o[:, columns(k, q)] * wg[:, columns(k, q)].astype(F32)
+                + up_o[:, columns(k, q)] * wu[:, columns(k, q)].astype(F32),
+                axis=0,
+                keepdims=True,
+            )
+            router_sums = jnp.dot(weights, normed, preferred_element_type=F32)
+            srb[0, yy, 2 * q + 1 : 2 * q + 2, group(k)] = router_sums[0:1] + router_sums[1:2]
+    for copy in st_copies(0):
+        copy.start()
+    hand_send_wait(bn, hn, 0)
+    hand_send_wait(bu, hu, 1)
+    ag_send_wait(gs, 0)
+    ag_send_wait(ss, 1)
+    for k in range(3):
+        a0[k][...] = rs_sum(k, 0).astype(BF16)
+        rs_start(k, 1)
+    srb[1, xx] = st_sum(0)
+    for copy in st_copies(1):
+        copy.start()
+
+    sums = [rs_sum(k, 1) for k in range(3)]
+    srb[2, zz] = st_sum(1)
+    for copy in st_copies(2):
+        copy.start()
     info, chance = tile_info()
     spare = sums[2][:, FEATS[2] :]
     logit_grad = (spare[:, 0:1] + spare[:, 1:2]) * (1.0 - chance)
@@ -533,6 +582,9 @@
     back_over_copy(yy).start()
     u[yy, 0:2] = new_tile[...]
     st_o[...] = st_sum(2)
+    for k in range(3):
+        for stage in range(2):
+            rs_all(k, stage).wait_send()
     for copy in back_copies():
         copy.wait_recv()
 
@@ -571,14 +623,6 @@
         nb_copy().wait_recv()
         nb_o[...] = nb[...]
 
-    hand_send_wait(bn, hn, 0)
-    hand_send_wait(bu, hu, 1)
-    ag_send_wait(gs, 0)
-    ag_send_wait(ss, 1)
-    for k in range(3):
-        for stage in range(3):
-            for copy in rs_copies(k, stage):
-                copy.wait_send()
     for copy in back_copies():
         copy.wait_send()
     back_over_copy(yy).wait_send()
@@ -617,17 +661,15 @@
         + [pltpu.VMEM(cube + (w,), BF16) for w in WIDTHS]
         + [pltpu.VMEM((3, RING, RING, ROWS, w), BF16) for w in WIDTHS]
         + [pltpu.VMEM((RING, RING, ROWS, w), BF16) for w in WIDTHS]
-        + [pltpu.VMEM((3, RING, ROWS, w), BF16) for w in WIDTHS]
-        + [pltpu.VMEM((RING, ROWS, w), BF16) for w in WIDTHS]
-        + [pltpu.VMEM((3, ROWS, w), BF16) for w in WIDTHS]
+        + [pltpu.VMEM((len(STEPS), ROWS, w), BF16) for w in WIDTHS]
         + [pltpu.VMEM((RING, 4, 8, width), BF16)]
         + [pltpu.VMEM((RING, 8, width), BF16)]
         + [pltpu.VMEM((3, RING, 8, width), F32)]
-        + [pltpu.VMEM((3, rows, ff), F32)]
+        + [pltpu.VMEM((5, rows, ff), F32)]
         + [pltpu.VMEM(wg.shape[1:], BF16)] * 3
         + [dma((2, 8)), dma((2, 4))]
-        + [dma((2, 3, 3, 4)), dma((2, 3, 3, 4))]
-        + [dma((3, 3, 4)), dma((3, 3, 4))]
+        + [dma((2, 3, 2)), dma((2, 3, 2))]
+        + [dma((3, 2)), dma((3, 2))]
         + [dma((3, 4)), dma((3, 4))]
         + [dma((4,)), dma((8,))]
         + [dma((3,)), dma((3,))]

time: 100 us -> 93.7 us (0.937)
  Pallas kernels: 98.7 us -> 92.9 us
    pallas_call x1, Pallas kernels: 93.5 us -> 87.7 us  [communicate(): pl.pallas_call(step_kernel, out_shape=out_shape, in_specs=[smem] * 2 + [h...]
where the time goes in v5:
time: 93.7 us; the launch traced here: 93.6 us
  Pallas kernels  92.9 us (99%)
    pallas_call x1, Pallas kernels, communicate(): pl.pallas_call(step_kernel, out_shape=out_shape, in_specs=[smem] * 2 + [h...  87.7 us
    pallas_call x1, Pallas kernels, finish(): pl.pallas_call(finish_kernel, out_shape=[shape((1, tok_rows, model_dim),...  5.22 us

profile of v5, /device:TPU:0, one launch (start us, length us, event | category | flops | bytes accessed | tf_op | source)
XLA Modules:
  0.0 93.6 jit_solution(7089229328688577534)
XLA Ops:
  0.6 0.0 copy-start.1
  0.6 0.0 copy-start
  0.7 87.7 %routed_step.1 = (f32[224,4096]{1,0:T(8,128)S(1)}, f32[224,4096]{1,0:T(8,128)S(1)}, f32[224,4096]{1,0:T(8,128)S(1)}, bf16[4,8,1152]{2,1,0:T(8,128)(2,1)S(1)}, bf...) custom-call(s32[1,1,2]{2,1,0:T(1,128)} %blocks.1, s32[1,1,2]{2,1,0:T(1,128)} %targets.1, ...), custom_call_target="tpu_custom_call" | custom-call | tf_op jit(solution)/shard_map/routed_step/pallas_call | solution.py:679
  88.3 0.0 copy-done.1
  88.3 0.0 copy-done
  88.3 5.2 %finish.1 = (bf16[1,128,4096]{2,1,0:T(8,128)(2,1)}, f32[1,224,4096]{2,1,0:T(8,128)}, f32[1,224,4096]{2,1,0:T(8,128)}, f32[1,224,4096]{2,1,0:T(8,128)}, f32[1,4096]{1,0:T(1,128)}, /*index=5*/f32[1,4096]{1,0:T(1,128)}) custom-call(f32[224,4096]{1,0:T(8,128)S(1)} %get-tuple-element.12.gate, f32[224,4096]{1,0:T(8,128)S(1)} %get-tuple-element.13.up, ...), custom_call_target="tpu_custom_call" | custom-call | tf_op jit(solution)/shard_map/finish/pallas_call | solution.py:739
Async XLA Ops:
  0.6 87.7 %copy-start.1 = (f32[1,4096]{1,0:T(1,128)S(1)}, f32[1,4096]{1,0:T(1,128)}, u32[]{:S(2)}) copy-start(f32[1,4096]{1,0:T(1,128)} %gain.1) | copy-start | bytes 49156
  0.6 87.7 %copy-start = (bf16[128,4096]{1,0:T(8,128)(2,1)S(1)}, bf16[128,4096]{1,0:T(8,128)(2,1)}, u32[]{:S(2)}) copy-start(bf16[128,4096]{1,0:T(8,128)(2,1)} %grad_hbm.3) | copy-start | bytes 3145732

commit v6 on v5

--- a/solution.py
+++ b/solution.py
@@ -15,6 +15,7 @@
 FEATS = (384, 384, 256)
 STARTS = (0, 384, 768)
 ROWS = 16
+PARTS = 4
 ALONG = (0, 1, 2)
 PLANES = ((1, 2), (0, 2), (0, 1))
 STEPS = tuple((i, j) for i in range(RING) for j in range(RING) if (i, j) != (0, 0))
@@ -35,9 +36,9 @@
 
 
 def step_kernel(
-    blocks, targets, saved_hbm, grad_hbm, gain_hbm, router_hbm, wg_hbm, wu_hbm, wd_hbm,
+    blocks_hbm, targets_hbm, saved_hbm, grad_hbm, gain_hbm, router_hbm, wg_hbm, wu_hbm, wd_hbm,
     gate_o, up_o, down_o, nb_o, new_o, st_o,
-    saved, grad_out, gain, router_row, gain_q, router_q, bn, bu, hn, hu, up_tile, new_tile,
+    blocks, targets, saved, grad_out, gain, router_row, gain_q, router_q, bn, bu, hn, hu, up_tile, new_tile,
     above, g0, g1, g2, s0, s1, s2, r0, r1, r2,
     rb00, rb01, rb02, a00, a01, a02, rb10, rb11, rb12,
     u, nb, srb, acc, wg, wu, wd,
@@ -56,19 +57,22 @@
     prev_base = lax.rem(quartet + quartets - 1, quartets) * RING
     prev_last = prev_base + RING - 1
 
+    ring = [[one] + [lax.rem(one + RING - off, RING) for off in OFFS] for one in at]
+    share = [[one * stride for one in row] for row, stride in zip(ring, (1, 16, 4))]
+
     def ring_index(dim, off):
-        return lax.rem(at[dim] + RING - off, RING)
+        return ring[dim][off]
 
     def peer(dim, off):
-        pos = list(at)
-        pos[dim] = ring_index(dim, off)
-        return {"pipe": pipe, "ctx": pos[1] * 16 + pos[2] * 4 + pos[0]}
+        parts = [row[0] for row in share]
+        parts[dim] = share[dim][off]
+        return {"pipe": pipe, "ctx": parts[0] + parts[1] + parts[2]}
 
     def plane_peer(k, step):
-        pos = list(at)
+        parts = [row[0] for row in share]
         for dim, off in zip(PLANES[k], step):
-            pos[dim] = ring_index(dim, off)
-        return {"pipe": pipe, "ctx": pos[1] * 16 + pos[2] * 4 + pos[0]}
+            parts[dim] = share[dim][off]
+        return {"pipe": pipe, "ctx": parts[0] + parts[1] + parts[2]}
 
     def same_pipe(ctx):
         return {"pipe": pipe, "ctx": ctx}
@@ -93,10 +97,11 @@
         pl.semaphore_signal(barrier, inc=1, device_id=device, device_id_type=MESH)
 
     row_copies = [
-        pltpu.make_async_copy(src, dst, local_sem.at[9 + i])
+        pltpu.make_async_copy(src, dst, local_sem.at[3 + i])
         for i, (src, dst) in enumerate(
             (
-                (saved_hbm.at[0], saved),
+                (blocks_hbm, blocks),
+                (targets_hbm, targets),
                 (gain_hbm, gain),
                 (router_hbm, router_row),
                 (grad_hbm, grad_out),
@@ -107,7 +112,15 @@
         pltpu.make_async_copy(src.at[0], dst, local_sem.at[i])
         for i, (src, dst) in enumerate(((wg_hbm, wg), (wu_hbm, wu), (wd_hbm, wd)))
     ]
-    for copy in row_copies:
+    saved_copies = [
+        pltpu.make_async_copy(
+            saved_hbm.at[0, :, pl.ds(q * QUARTER, QUARTER)],
+            saved.at[:, pl.ds(q * QUARTER, QUARTER)],
+            local_sem.at[8 + q],
+        )
+        for q in range(RING)
+    ]
+    for copy in row_copies[:2] + saved_copies + row_copies[2:]:
         copy.start()
     for dim in range(3):
         for off in OFFS:
@@ -124,6 +137,8 @@
         for j in range(RING):
             greet(same_pipe(next_base + j))
 
+    for copy in row_copies[:2]:
+        copy.wait()
     kept = targets[0, 0, 0] == me
     keep_block = jnp.where(kept, blocks[0, 0, 0], blocks[0, 0, 1])
     hand_block = jnp.where(kept, blocks[0, 0, 1], blocks[0, 0, 0])
@@ -143,12 +158,13 @@
     def quarter(q):
         return slice(q * QUARTER, (q + 1) * QUARTER)
 
-    for copy in row_copies[:3]:
+    for copy in row_copies[2:4]:
         copy.wait()
     squares = jnp.zeros((2 * BLOCK, 1), F32)
     logits = jnp.zeros((2 * BLOCK, 1), F32)
     picked = []
     for q in range(RING):
+        saved_copies[q].wait()
         rows = pick(saved, quarter(q))
         picked.append(rows)
         gain_q[q] = gain[:, quarter(q)]
@@ -282,7 +298,7 @@
             ag_start(bufs, which, k, 1)
 
     hand_start(bn, hn, 0)
-    row_copies[3].wait()
+    row_copies[4].wait()
     for q in range(RING):
         bu[q] = pick(grad_out, quarter(q)).astype(BF16)
     hand_start(bu, hu, 1)
@@ -352,12 +368,15 @@
     acc[4] = acc[1] * sigma * (1.0 + gate_pre * (1.0 - sigma))
 
     def above_copies():
-        return [
+        whole = remote(
+            new_tile, above.at[1], ab_send.at[1], ab_recv.at[1], other_pipe(me)
+        )
+        return [whole] + [
             remote(
-                new_tile, above.at[slot], ab_send.at[slot], ab_recv.at[slot],
+                new_tile.at[h], above.at[slot, h], ab_send.at[slot], ab_recv.at[slot],
                 other_pipe(base + yy),
             )
-            for slot, base in ((2, prev_base), (1, quartet * RING), (0, next_base))
+            for slot, h, base in ((2, 0, prev_base), (0, 1, next_base))
         ]
 
     @pl.when(pipe == 0)
@@ -539,9 +558,6 @@
         copy.start()
 
     sums = [rs_sum(k, 1) for k in range(3)]
-    srb[2, zz] = st_sum(1)
-    for copy in st_copies(2):
-        copy.start()
     info, chance = tile_info()
     spare = sums[2][:, FEATS[2] :]
     logit_grad = (spare[:, 0:1] + spare[:, 1:2]) * (1.0 - chance)
@@ -573,15 +589,17 @@
 
     def back_over_copy(q):
         return remote(
-            new_tile, u.at[q, pl.ds(2, 2)], un_send.at[0], un_recv.at[RING + q],
+            new_tile.at[0], u.at[q, 2], un_send.at[0], un_recv.at[RING + q],
             same_pipe(prev_last),
         )
 
     for copy in back_copies():
         copy.start()
     back_over_copy(yy).start()
+    srb[2, zz] = st_sum(1)
+    for copy in st_copies(2):
+        copy.start()
     u[yy, 0:2] = new_tile[...]
-    st_o[...] = st_sum(2)
     for k in range(3):
         for stage in range(2):
             rs_all(k, stage).wait_send()
@@ -610,6 +628,8 @@
         new_o[q, :, :QUARTER] = owned(q, slice(0, QUARTER)).astype(BF16)
         new_o[q, :, QUARTER:] = which.astype(BF16)
 
+    st_o[...] = st_sum(2)
+
     def nb_copy():
         return remote(new_o, nb, nb_send, nb_recv, other_pipe(me))
 
@@ -639,7 +659,6 @@
     rows = RING * RING * ROWS
     width = QUARTER + EXTRA
     vmem = pl.BlockSpec(memory_space=pltpu.VMEM)
-    smem = pl.BlockSpec(memory_space=pltpu.SMEM)
     hbm = pl.BlockSpec(memory_space=pl.ANY)
     cube = (RING, RING, RING, ROWS)
     out_shape = (
@@ -649,7 +668,8 @@
     )
     dma = pltpu.SemaphoreType.DMA
     scratch = (
-        [pltpu.VMEM(grad_out.shape, BF16)] * 2
+        [pltpu.SMEM(route_blocks.shape, jnp.int32)] * 2
+        + [pltpu.VMEM(grad_out.shape, BF16)] * 2
         + [pltpu.VMEM(gain.shape, F32), pltpu.VMEM(w_router.shape, BF16)]
         + [pltpu.VMEM((RING, 1, QUARTER), F32)] * 2
         + [pltpu.VMEM((RING, 8, width), BF16), pltpu.VMEM((RING, 8, QUARTER), BF16)]
@@ -662,7 +682,7 @@
         + [pltpu.VMEM((3, RING, RING, ROWS, w), BF16) for w in WIDTHS]
         + [pltpu.VMEM((RING, RING, ROWS, w), BF16) for w in WIDTHS]
         + [pltpu.VMEM((len(STEPS), ROWS, w), BF16) for w in WIDTHS]
-        + [pltpu.VMEM((RING, 4, 8, width), BF16)]
+        + [pltpu.VMEM((RING, 3, 8, width), BF16)]
         + [pltpu.VMEM((RING, 8, width), BF16)]
         + [pltpu.VMEM((3, RING, 8, width), F32)]
         + [pltpu.VMEM((5, rows, ff), F32)]
@@ -679,7 +699,7 @@
     return pl.pallas_call(
         step_kernel,
         out_shape=out_shape,
-        in_specs=[smem] * 2 + [hbm] * 7,
+        in_specs=[hbm] * 9,
         out_specs=[vmem] * 6,
         scratch_shapes=scratch,
         compiler_params=pltpu.CompilerParams(
@@ -696,9 +716,14 @@
 ):
     load = pltpu.make_async_copy(grad_hbm, grad_out, sem.at[0])
     load.start()
+    part = gate.shape[0] // PARTS
     copies = [
-        pltpu.make_async_copy(src, dst.at[0], sem.at[1 + i])
+        pltpu.make_async_copy(
+            src.at[pl.ds(j * part, part)], dst.at[0, pl.ds(j * part, part)],
+            sem.at[2 + i * PARTS + j],
+        )
         for i, (src, dst) in enumerate(((gate, out_gate), (up, out_up), (down, out_down)))
+        for j in range(PARTS)
     ]
     for copy in copies:
         copy.start()
@@ -724,7 +749,7 @@
             for which, pattern in patterns:
                 value = jnp.where(block == which, pattern, value)
             outcome[8 * i : 8 * i + 8, cols] = value.astype(BF16)
-    store = pltpu.make_async_copy(outcome, out_inputs.at[0], sem.at[4])
+    store = pltpu.make_async_copy(outcome, out_inputs.at[0], sem.at[1])
     store.start()
     for copy in copies + [store]:
         copy.wait()
@@ -744,7 +769,7 @@
         in_specs=[vmem] * 3 + [hbm] + [vmem] * 4,
         out_specs=[hbm] * 4 + [vmem] * 2,
         scratch_shapes=[pltpu.VMEM(grad_out.shape, BF16)] * 2
-        + [pltpu.SemaphoreType.DMA((5,))],
+        + [pltpu.SemaphoreType.DMA((2 + 3 * PARTS,))],
         compiler_params=pltpu.CompilerParams(vmem_limit_bytes=8 * 1024 * 1024),
         name="finish",
     )(gate, up, down, grad_out, nb, fresh, stats, gain)

time: 93.7 us -> 92.6 us (0.988)
  Pallas kernels: 92.9 us -> 91.8 us
    pallas_call x1, Pallas kernels: 87.7 us -> 86.6 us  [communicate(): pl.pallas_call(step_kernel, out_shape=out_shape, in_specs=[hbm] * 9, out_...]
where the time goes in v6:
time: 92.6 us; the launch traced here: 92.5 us
  Pallas kernels  91.8 us (99%)
    pallas_call x1, Pallas kernels, communicate(): pl.pallas_call(step_kernel, out_shape=out_shape, in_specs=[hbm] * 9, out_...  86.6 us
    pallas_call x1, Pallas kernels, finish(): pl.pallas_call(finish_kernel, out_shape=[shape((1, tok_rows, model_dim),...  5.22 us

profile of v6, /device:TPU:0, one launch (start us, length us, event | category | flops | bytes accessed | tf_op | source)
XLA Modules:
  0.0 92.5 jit_solution(16582189548443299911)
XLA Ops:
  0.6 0.0 copy-start.1
  0.6 0.0 copy-start
  0.7 86.6 %routed_step.1 = (f32[224,4096]{1,0:T(8,128)S(1)}, f32[224,4096]{1,0:T(8,128)S(1)}, f32[224,4096]{1,0:T(8,128)S(1)}, bf16[4,8,1152]{2,1,0:T(8,128)(2,1)S(1)}, bf...) custom-call(s32[1,1,2]{2,1,0:T(1,128)} %blocks_hbm.1, s32[1,1,2]{2,1,0:T(1,128)} %targets_hbm.1, ...), custom_call_target="tpu_custom_call" | custom-call | tf_op jit(solution)/shard_map/routed_step/pallas_call | solution.py:699
  87.3 0.0 copy-done.1
  87.3 0.0 copy-done
  87.3 5.2 %finish.1 = (bf16[1,128,4096]{2,1,0:T(8,128)(2,1)}, f32[1,224,4096]{2,1,0:T(8,128)}, f32[1,224,4096]{2,1,0:T(8,128)}, f32[1,224,4096]{2,1,0:T(8,128)}, f32[1,4096]{1,0:T(1,128)}, /*index=5*/f32[1,4096]{1,0:T(1,128)}) custom-call(f32[224,4096]{1,0:T(8,128)S(1)} %get-tuple-element.12.gate, f32[224,4096]{1,0:T(8,128)S(1)} %get-tuple-element.13.up, ...), custom_call_target="tpu_custom_call" | custom-call | tf_op jit(solution)/shard_map/finish/pallas_call | solution.py:764
Async XLA Ops:
  0.6 86.6 %copy-start.1 = (f32[1,4096]{1,0:T(1,128)S(1)}, f32[1,4096]{1,0:T(1,128)}, u32[]{:S(2)}) copy-start(f32[1,4096]{1,0:T(1,128)} %gain.1) | copy-start | bytes 49156
  0.6 86.6 %copy-start = (bf16[128,4096]{1,0:T(8,128)(2,1)S(1)}, bf16[128,4096]{1,0:T(8,128)(2,1)}, u32[]{:S(2)}) copy-start(bf16[128,4096]{1,0:T(8,128)(2,1)} %grad_hbm.3) | copy-start | bytes 3145732

commit v7 on v6

--- a/solution.py
+++ b/solution.py
@@ -423,13 +423,13 @@
         make_scaled()
         go_on(ss, 1)
 
-    for k in range(3):
+    for k in (2, 0, 1):
         ag_recv_wait(ss, 1, k, 1)
         grad_sum = None
         for q in range(RING):
             part = contract_last(rows_of(ss, k, q), wd[:, columns(k, q)])
             grad_sum = part if grad_sum is None else grad_sum + part
-        if k == 0:
+        if k == 2:
             acc[2] = grad_sum
         else:
             acc[2] += grad_sum
@@ -439,19 +439,8 @@
     hidden_grad = acc[2]
     activated = acc[3]
     hidden = (activated * up_value).astype(BF16)
-    row_part = jnp.sum(hidden_grad * hidden.astype(F32), axis=1, keepdims=True)
     gg = (hidden_grad * acc[4]).astype(BF16)
     ug = (hidden_grad * activated).astype(BF16)
-    dot_part = jnp.sum(
-        gg.astype(F32) * gate_pre + ug.astype(F32) * up_value, axis=1, keepdims=True
-    )
-    extra = g2[0, :, :, :, FEATS[2] :].reshape(quartets * ROWS, EXTRA).astype(F32)
-    lane = lax.broadcasted_iota(jnp.int32, (quartets * ROWS, EXTRA), 1)
-    row_lanes = jnp.zeros((quartets * ROWS, EXTRA), F32)
-    for i, value in enumerate(hi_lo(row_part) + hi_lo(dot_part)):
-        row_lanes = jnp.where(lane == i, value, row_lanes)
-    row_lanes = row_lanes.astype(BF16).reshape(RING, RING, ROWS, EXTRA)
-
     def rs_copies(k, stage):
         if stage == 0:
             copies = []
@@ -499,6 +488,17 @@
 
     srb[0, yy] = jnp.zeros((2 * RING, QUARTER + EXTRA), F32)
     for k in range(3):
+        if k == 2:
+            row_part = jnp.sum(hidden_grad * hidden.astype(F32), axis=1, keepdims=True)
+            dot_part = jnp.sum(
+                gg.astype(F32) * gate_pre + ug.astype(F32) * up_value, axis=1, keepdims=True
+            )
+            extra = g2[0, :, :, :, FEATS[2] :].reshape(quartets * ROWS, EXTRA).astype(F32)
+            lane = lax.broadcasted_iota(jnp.int32, (quartets * ROWS, EXTRA), 1)
+            row_lanes = jnp.zeros((quartets * ROWS, EXTRA), F32)
+            for i, value in enumerate(hi_lo(row_part) + hi_lo(dot_part)):
+                row_lanes = jnp.where(lane == i, value, row_lanes)
+            row_lanes = row_lanes.astype(BF16).reshape(RING, RING, ROWS, EXTRA)
         for q in range(RING):
             part = jnp.dot(gg, wg[:, columns(k, q)], preferred_element_type=F32) + jnp.dot(
                 ug, wu[:, columns(k, q)], preferred_element_type=F32

time: 92.6 us -> 91.8 us (level)
  no operation moved by 1% of the time
where the time goes in v7:
time: 91.8 us; the launch traced here: 91.7 us
  Pallas kernels  91 us (99%)
    pallas_call x1, Pallas kernels, communicate(): pl.pallas_call(step_kernel, out_shape=out_shape, in_specs=[hbm] * 9, out_...  85.8 us
    pallas_call x1, Pallas kernels, finish(): pl.pallas_call(finish_kernel, out_shape=[shape((1, tok_rows, model_dim),...  5.22 us

profile of v7, /device:TPU:0, one launch (start us, length us, event | category | flops | bytes accessed | tf_op | source)
XLA Modules:
  0.0 91.7 jit_solution(6452084432113574405)
XLA Ops:
  0.6 0.0 copy-start.1
  0.6 0.0 copy-start
  0.7 85.8 %routed_step.1 = (f32[224,4096]{1,0:T(8,128)S(1)}, f32[224,4096]{1,0:T(8,128)S(1)}, f32[224,4096]{1,0:T(8,128)S(1)}, bf16[4,8,1152]{2,1,0:T(8,128)(2,1)S(1)}, bf...) custom-call(s32[1,1,2]{2,1,0:T(1,128)} %blocks_hbm.1, s32[1,1,2]{2,1,0:T(1,128)} %targets_hbm.1, ...), custom_call_target="tpu_custom_call" | custom-call | tf_op jit(solution)/shard_map/routed_step/pallas_call | solution.py:699
  86.4 0.0 copy-done.1
  86.4 0.0 copy-done
  86.4 5.2 %finish.1 = (bf16[1,128,4096]{2,1,0:T(8,128)(2,1)}, f32[1,224,4096]{2,1,0:T(8,128)}, f32[1,224,4096]{2,1,0:T(8,128)}, f32[1,224,4096]{2,1,0:T(8,128)}, f32[1,4096]{1,0:T(1,128)}, /*index=5*/f32[1,4096]{1,0:T(1,128)}) custom-call(f32[224,4096]{1,0:T(8,128)S(1)} %get-tuple-element.12.gate, f32[224,4096]{1,0:T(8,128)S(1)} %get-tuple-element.13.up, ...), custom_call_target="tpu_custom_call" | custom-call | tf_op jit(solution)/shard_map/finish/pallas_call | solution.py:764
Async XLA Ops:
  0.6 85.8 %copy-start.1 = (f32[1,4096]{1,0:T(1,128)S(1)}, f32[1,4096]{1,0:T(1,128)}, u32[]{:S(2)}) copy-start(f32[1,4096]{1,0:T(1,128)} %gain.1) | copy-start | bytes 49156
  0.6 85.8 %copy-start = (bf16[128,4096]{1,0:T(8,128)(2,1)S(1)}, bf16[128,4096]{1,0:T(8,128)(2,1)}, u32[]{:S(2)}) copy-start(bf16[128,4096]{1,0:T(8,128)(2,1)} %grad_hbm.3) | copy-start | bytes 3145732
